TPU v7x, 32 devices: a whole 2x2x4 slice. The times are simulated.
32 devices in a mesh: row: 8 (over z, y), col: 4 (over x, core).
Axes of the slice: x: 2, y: 2, z: 4, core: 2. Of those that a mesh axis runs over, the one named last changes fastest.
Arguments:
- relation: float32 [16384, 16384], P('row', 'col'), as said below
- dosage: int32 [512, 16384], P(None, 'col'), may hold values from 0 to 200
- freq: int32 [512], replicated, may hold values from 500 to 9500
- panel: int32 [1], replicated, may hold values from 0 to 502
Outputs:
- reduced: float32 [16384, 16384], P('row', 'col')
Inputs may be any that keep to these rules, and one draw needn't show every extreme that they name: relation is symmetric.
All inputs are finite; a program needn't handle non-finite values.
Results may differ from a plain program's by a relative error of at most 0.00045.
Values may be sent and summed in bfloat16 or wider, within the bound.
No kernel may reach another device: no remote copies, remote signals or barrier semaphores. Data moves between devices by JAX's collectives and lax.ppermute only.
A program may use at most 192 MiB of HBM per device.

v0:
```python
import jax
import jax.numpy as jnp
from jax import lax
from jax.sharding import PartitionSpec as P

B = 32
M = 512


HIGH = lax.Precision.HIGHEST


def spread_2(value, axis, source):
    kept = jnp.where(lax.axis_index(axis) == source, value, 0).astype(value.dtype)
    return lax.psum(kept, axis)


def standardize(dosage, freq):
    allele = freq.astype(jnp.float32) / 10000.0
    spread = jnp.sqrt(2.0 * allele * (1.0 - allele))
    scaled = (dosage.astype(jnp.float32) / 100.0 - 2.0 * allele[:, None]) / spread[:, None]
    return scaled.astype(jnp.bfloat16)


def householder(panel_block, first_row):
    height = panel_block.shape[0]
    breadth = panel_block.shape[1]
    row_ids = jnp.arange(height, dtype=jnp.int32)
    slots = jnp.arange(breadth, dtype=jnp.int32)

    def reflect_step(column_id, carry):
        panel_work, vectors, triangle = carry
        pivot = first_row + column_id
        column = jnp.sum(jnp.where(slots[None, :] == column_id, panel_work, 0.0), axis=1)
        below = jnp.where(row_ids >= pivot, column, 0.0)
        at_pivot = row_ids == pivot
        alpha = jnp.sum(jnp.where(at_pivot, column, 0.0))
        length = jnp.sqrt(jnp.sum(below * below))
        signum = jnp.where(alpha >= 0.0, 1.0, -1.0)
        vector = below + jnp.where(at_pivot, signum * length, 0.0)
        scale_tau = 2.0 / jnp.sum(vector * vector)
        project = jnp.dot(vector, panel_work, precision=HIGH)
        panel_work = panel_work - scale_tau * vector[:, None] * project[None, :]
        cross = jnp.dot(vector, vectors, precision=HIGH)
        new_column = -scale_tau * jnp.dot(triangle, cross, precision=HIGH)
        picked = jnp.where(slots == column_id, 1.0, 0.0).astype(panel_work.dtype)
        triangle = (
            triangle
            + new_column[:, None] * picked[None, :]
            + scale_tau * picked[:, None] * picked[None, :]
        )
        vectors = vectors + vector[:, None] * picked[None, :]
        return (panel_work, vectors, triangle)

    start = (
        panel_block,
        jnp.zeros_like(panel_block),
        jnp.zeros((breadth, breadth), panel_block.dtype),
    )
    return lax.fori_loop(0, breadth, reflect_step, start)


def cholesky_lower(matrix):
    breadth = matrix.shape[0]
    slots = jnp.arange(breadth, dtype=jnp.int32)

    def column_step(column_id, factor):
        picked = jnp.where(slots == column_id, 1.0, 0.0).astype(jnp.float32)
        factor_row = jnp.dot(picked, factor, precision=HIGH)
        matrix_col = jnp.dot(matrix, picked, precision=HIGH)
        partial_value = matrix_col - jnp.dot(factor, factor_row, precision=HIGH)
        pivot_value = jnp.sum(partial_value * picked)
        root = jnp.sqrt(pivot_value)
        column = jnp.where(slots > column_id, partial_value / root, 0.0) + picked * root
        return factor + column[:, None] * picked[None, :]

    return lax.fori_loop(0, breadth, column_step, jnp.zeros((breadth, breadth), jnp.float32))


def solve_lower(lower, rhs):
    breadth = lower.shape[0]
    slots = jnp.arange(breadth, dtype=jnp.int32)

    def row_step(row_id, solved):
        picked = jnp.where(slots == row_id, 1.0, 0.0).astype(jnp.float32)
        lower_row = jnp.dot(picked, lower, precision=HIGH)
        diag_value = jnp.sum(lower_row * picked)
        rhs_row = jnp.dot(picked, rhs, precision=HIGH)
        value_row = (rhs_row - jnp.dot(lower_row, solved, precision=HIGH)) / diag_value
        return solved + picked[:, None] * value_row[None, :]

    return lax.fori_loop(0, breadth, row_step, jnp.zeros_like(rhs))


def body(relation, dosage, freq, panel):
    tile_rows, tile_cols = relation.shape
    row_id = lax.axis_index("row")
    col_id = lax.axis_index("col")
    row_start = row_id * tile_rows
    col_start = col_id * tile_cols
    owner_col = row_start // tile_cols
    inner_offset = row_start % tile_cols
    scaled = standardize(dosage, freq)
    own_dosage = lax.dynamic_slice_in_dim(scaled, inner_offset, tile_rows, 1)
    dosage_rows = spread_2(own_dosage, "col", owner_col)
    gram_tile = lax.dot_general(
        dosage_rows, scaled, (((0,), (0,)), ((), ())), preferred_element_type=jnp.float32
    )
    grown = relation + gram_tile / M
    panel_index = panel[0]
    first_row = (panel_index + 1) * B
    bottom_row = first_row + B
    strip_local = lax.dynamic_slice_in_dim(grown, panel_index * B % tile_rows, B, 0)
    strip_cols = spread_2(strip_local, "row", panel_index * B // tile_rows)
    col_ids = col_start + jnp.arange(tile_cols, dtype=jnp.int32)
    row_ids = row_start + jnp.arange(tile_rows, dtype=jnp.int32)
    slots = jnp.arange(B, dtype=jnp.int32)
    bottom_part = jnp.where(col_ids[None, :] >= bottom_row, strip_cols, 0.0)
    partial_cov = jnp.dot(bottom_part, bottom_part.T, precision=HIGH)
    top_select = jnp.where(col_ids[None, :] - first_row == slots[:, None], 1.0, 0.0)
    partial_top = jnp.dot(strip_cols, top_select.T, precision=HIGH)
    own_rows = lax.dynamic_slice_in_dim(strip_cols, inner_offset, tile_rows, 1)
    own_rows = jnp.where(col_id == owner_col, own_rows, 0.0)
    bottom_cov, top_trans, rows_trans = lax.psum((partial_cov, partial_top, own_rows), "col")
    stacked = jnp.concatenate([top_trans.T, cholesky_lower(bottom_cov).T], axis=0)
    panel_work, small_vectors, triangle = householder(stacked, 0)
    coupling = jnp.dot(
        triangle.T, jnp.dot(small_vectors.T, stacked, precision=HIGH), precision=HIGH
    )
    coupling_lower = coupling.T
    r_factor = jnp.triu(panel_work[:B])

    def reflectors(panel_trans, global_ids):
        select = jnp.where(global_ids[None, :] - first_row == slots[:, None], 1.0, 0.0)
        lifted = jnp.where(global_ids[None, :] >= first_row, panel_trans, 0.0) - jnp.dot(
            r_factor.T, select, precision=HIGH
        )
        return solve_lower(coupling_lower, lifted)

    vecs_cols = reflectors(strip_cols, col_ids)
    vecs_rows = reflectors(rows_trans, row_ids)
    sums_cols = lax.psum(jnp.dot(vecs_rows, grown, precision=HIGH), "row")
    applied_cols = jnp.dot(triangle.T, sums_cols, precision=HIGH)
    part_inner = jnp.dot(vecs_cols, applied_cols.T, precision=HIGH)
    part_rows = lax.dot_general(vecs_cols, grown, (((1,), (1,)), ((), ())), precision=HIGH)
    sums_rows, inner = lax.psum((part_rows, part_inner), "col")
    applied_rows = jnp.dot(triangle.T, sums_rows, precision=HIGH)
    middle = jnp.dot(triangle.T, inner, precision=HIGH)
    adjusted_cols = applied_cols - 0.5 * jnp.dot(middle.T, vecs_cols, precision=HIGH)
    adjusted_rows = applied_rows - 0.5 * jnp.dot(middle.T, vecs_rows, precision=HIGH)
    left_side = jnp.concatenate([vecs_rows, adjusted_rows], axis=0)
    right_side = jnp.concatenate([adjusted_cols, vecs_cols], axis=0)
    update = lax.dot_general(left_side, right_side, (((0,), (0,)), ((), ())), precision=HIGH)
    return grown - update


def solution(mesh):
    placed = (P("row", "col"), P(None, "col"), P(), P())
    return jax.shard_map(
        body, mesh=mesh, in_specs=placed, out_specs=P("row", "col"), check_vma=False
    )
```

profile of v0, /device:TPU:0, one launch (start us, length us, event | category | flops | bytes accessed | tf_op | source)
XLA Modules:
  0.0 737.6 jit_solution(5662830344409382923)
XLA Ops:
  7.2 4.4 divide_convert_fusion
  11.6 1.9 copy-done
  13.5 1.7 dynamic-slice_select_fusion
  16.0 53.5 %all-reduce.7.cloned.1.call-done = bf16[512,2048]{1,0:T(8,128)(2,1)} async-done(((bf16[512,2048]{1,0:T(8,128)(2,1)}), bf16[512,2048]{1,0:T(8,128)(2,1)}) %all-reduce.7.cloned.1.call-update) | async-done | bytes 2097168 | tf_op jit(solution)/shard_map/psum | solution.py:15
  69.5 28.8 %multiply_add_fusion.5 = f32[2048,4096]{1,0:T(8,128)} fusion(f32[2048,4096]{1,0:T(8,128)} %param.12, bf16[512,2048]{1,0:T(8,128)(2,1)} %all-reduce.7.cloned.1.call-done, bf16[512,4096]{1,0:T(8,128)(2,1)} %copy-done), kind=kOutput, calls=%fused_computation.83 | convolution fusion | flops 8606711808 | bytes 73400320 | tf_op jit(solution)/shard_map/dot_general | solution.py:106
  98.4 2.0 dynamic-slice_select_fusion.1
  100.5 72.8 %all-reduce.9.cloned.1.call-done = f32[32,4096]{1,0:T(8,128)} async-done(((f32[32,4096]{1,0:T(8,128)}), f32[32,4096]{1,0:T(8,128)}) %all-reduce.9.cloned.1.call-update) | async-done | bytes 524304 | tf_op jit(solution)/shard_map/psum | solution.py:15
  173.2 1.6 fusion.63
  174.9 1.8 fusion.68
  176.7 10.5 %all-reduce = (f32[32,32]{1,0:T(8,128)S(1)}, f32[32,32]{1,0:T(8,128)S(1)}) all-reduce(f32[32,32]{1,0:T(8,128)S(1)} %fusion.68, f32[32,32]{1,0:T(8,128)S(1)} %fusion.63), channel_id=1, replica_groups=mesh['row'=8,'col'=4] {'col'}, use_global_device_ids=true, to_apply=%region_3.4 | all-reduce | flops 2048 | bytes 16384 | tf_op jit(solution)/shard_map/psum | solution.py:124
  187.2 59.9 %while.64 = (s32[]{:T(128)}, f32[32,32]{1,0:T(8,128)S(1)}, f32[32,32]{1,0:T(8,128)S(1)}, s32[]{:T(128)}, s32[]{:T(128)}) while((s32[]{:T(128)}, f32[32,32]{1,0:T(8,128)S(1)}, f32[32,32]{1,0:T(8,128)S(1)}, s32[]{:T(128)}, s32[]{:T(128)}) %tuple.141), condition=%wide.region_6.7_spmd.clone.clone, body=%wide.region_4.6_spmd.clone.clone.sunk | while | flops 42498 | bytes 21865 | solution.py:77
  187.4 0.8 multiply_reduce_fusion.6
  189.3 0.8 multiply_reduce_fusion.6
  191.2 0.8 multiply_reduce_fusion.6
  193.1 0.8 multiply_reduce_fusion.6
  194.9 0.8 multiply_reduce_fusion.6
  196.8 0.8 multiply_reduce_fusion.6
  198.7 0.8 multiply_reduce_fusion.6
  200.5 0.8 multiply_reduce_fusion.6
  202.4 0.8 multiply_reduce_fusion.6
  204.3 0.8 multiply_reduce_fusion.6
  206.2 0.8 multiply_reduce_fusion.6
  208.0 0.8 multiply_reduce_fusion.6
  209.9 0.8 multiply_reduce_fusion.6
  211.8 0.8 multiply_reduce_fusion.6
  213.6 0.8 multiply_reduce_fusion.6
  215.5 0.8 multiply_reduce_fusion.6
  217.4 0.8 multiply_reduce_fusion.6
  219.2 0.8 multiply_reduce_fusion.6
  221.1 0.8 multiply_reduce_fusion.6
  223.0 0.8 multiply_reduce_fusion.6
  224.9 0.8 multiply_reduce_fusion.6
  226.7 0.8 multiply_reduce_fusion.6
  228.6 0.8 multiply_reduce_fusion.6
  230.5 0.8 multiply_reduce_fusion.6
  232.3 0.8 multiply_reduce_fusion.6
  234.2 0.8 multiply_reduce_fusion.6
  236.1 0.8 multiply_reduce_fusion.6
  237.9 0.8 multiply_reduce_fusion.6
  239.8 0.8 multiply_reduce_fusion.6
  241.7 0.8 multiply_reduce_fusion.6
  243.6 0.8 multiply_reduce_fusion.6
  245.4 0.8 multiply_reduce_fusion.6
  247.1 130.0 %while.65 = (s32[]{:T(128)}, f32[64,32]{1,0:T(8,128)S(1)}, f32[64,32]{1,0:T(8,128)S(1)}, f32[32,32]{1,0:T(8,128)S(1)}, s32[]{:T(128)}, /*index=5*/f32[]{:T(128)}, f32[]{:T(128)}, f32[]{:T(128)}, s32[]{:T(128)}, f32[]{:T(128)}) while((s32[]{:T(128)}, f32[64,32]{1,0:T(8,128)S(1)}, f32[64,32]{1,0:T(8,128)S(1)}, ...), condition=%wide.region_12.13_spmd.clone.clone, body=%wide.region_7.12_spmd.clone.clone.sunk | while | flops 85093 | bytes 73888 | solution.py:60
  377.6 1.8 convolution_subtract_fusion.1
  379.4 70.3 %while.63 = (s32[]{:T(128)}, f32[32,4096]{1,0:T(8,128)S(1)}, f32[32,4096]{1,0:T(8,128)S(1)}, f32[32,32]{1,0:T(8,128)S(1)}, s32[]{:T(128)}, /*index=5*/s32[]{:T(128)}) while((s32[]{:T(128)}, f32[32,4096]{1,0:T(8,128)S(1)}, f32[32,4096]{1,0:T(8,128)S(1)}, f32[32,32]{1,0:T(8,128)S(1)}, s32[]{:T(128)}, /*index=5*/s32[]{:T(128)}) %tuple.147), condition=%wide.region_19.20_spmd.clone, body=%wide.region_17.19_spmd.clone.sunk | while | flops 3690818 | bytes 2200164 | solution.py:92
  449.7 34.4 %fusion.102 = f32[32,2048]{1,0:T(8,128)} fusion(f32[32,4096]{1,0:T(8,128)S(1)} %get-tuple-element.394, f32[2048,4096]{1,0:T(8,128)} %multiply_add_fusion.5), kind=kOutput, calls=%fused_computation.147 | convolution fusion | flops 3221225472 | bytes 34340864 | tf_op jit(solution)/shard_map/dot_general | solution.py:145
  485.1 32.5 %all-reduce.13.cloned.1.call-done = (f32[32,2048]{1,0:T(8,128)}, f32[32,2048]{1,0:T(8,128)}) async-done(((f32[32,2048]{1,0:T(8,128)}, f32[32,2048]{1,0:T(8,128)}), (f32[32,2048]{1,0:T(8,128)}, f32[32,2048]{1,0:T(8,128)})) %all-reduce.13.cloned.1.call-update) | async-done | bytes 524304 | tf_op jit(solution)/shard_map/psum | solution.py:124
  517.6 1.4 convolution_subtract_fusion.2
  519.1 68.7 %while.62 = (s32[]{:T(128)}, f32[32,2048]{1,0:T(8,128)S(1)}, f32[32,2048]{1,0:T(8,128)S(1)}, f32[32,32]{1,0:T(8,128)S(1)}, s32[]{:T(128)}, /*index=5*/s32[]{:T(128)}) while((s32[]{:T(128)}, f32[32,2048]{1,0:T(8,128)S(1)}, f32[32,2048]{1,0:T(8,128)S(1)}, f32[32,32]{1,0:T(8,128)S(1)}, s32[]{:T(128)}, /*index=5*/s32[]{:T(128)}) %tuple.162), condition=%wide.region_16.17_spmd.clone, body=%wide.region_14.16_spmd.clone.sunk | while | flops 1851714 | bytes 1102436 | solution.py:92
  519.1 0.8 fusion.172
  523.4 0.8 fusion.172
  525.5 0.8 fusion.172
  529.8 0.8 fusion.172
  532.0 0.8 fusion.172
  534.1 0.8 fusion.172
  536.3 0.8 fusion.172
  538.4 0.8 fusion.172
  540.6 0.8 fusion.172
  587.8 23.7 %fusion.104 = f32[32,4096]{1,0:T(8,128)} fusion(f32[32,2048]{1,0:T(8,128)S(1)} %get-tuple-element.393, f32[2048,4096]{1,0:T(8,128)} %multiply_add_fusion.5), kind=kOutput, calls=%fused_computation.149 | convolution fusion | flops 3221225472 | bytes 34340864 | tf_op jit(solution)/shard_map/dot_general | solution.py:142
  611.9 72.5 %all-reduce.11.cloned.1.call-done = f32[32,4096]{1,0:T(8,128)} async-done(((f32[32,4096]{1,0:T(8,128)}), f32[32,4096]{1,0:T(8,128)}) %all-reduce.11.cloned.1.call-update) | async-done | bytes 524304 | tf_op jit(solution)/shard_map/psum | solution.py:142
  684.5 1.7 fusion.105
  686.7 10.1 %psum.63 = f32[32,32]{1,0:T(8,128)S(1)} all-reduce(f32[32,32]{1,0:T(8,128)S(1)} %fusion.106), channel_id=1, replica_groups=mesh['row'=8,'col'=4] {'col'}, use_global_device_ids=true, to_apply=%region_22.23 | all-reduce | flops 1024 | bytes 8192 | tf_op jit(solution)/shard_map/psum | solution.py:146
  698.1 32.9 %convolution_subtract_fusion = f32[2048,4096]{1,0:T(8,128)} fusion(f32[2048,4096]{1,0:T(8,128)} %multiply_add_fusion.5, f32[32,4096]{1,0:T(8,128)S(1)} %get-tuple-element.394, f32[32,4096]{1,0:T(8,128)S(1)} %fusion.57, f32[32,2048]{1,0:T(8,128)S(1)} %fusion.58, f32[32,2048]{1,0:T(8,128)S(1)} %get-tuple-element.393), kind=kOutput, calls=%fused_computation.84 | convolution fusion | flops 6451232768 | bytes 68681728 | tf_op jit(solution)/shard_map/dot_general | solution.py:153
  (922 shorter events, 209.4 us)
Async XLA Ops:
  6.5 63.0 %all-reduce.7.cloned.1.call-start = ((), (), s32[]{:S(2)}) async-start(), calls=%async_computation | async-start | bytes 4194304 | tf_op jit(solution)/shard_map/psum | solution.py:15
  11.6 1.9 copy-start
  15.3 158.0 %all-reduce.9.cloned.1.call-start = ((), (), s32[]{:S(2)}) async-start(), calls=%async_computation.1 | async-start | bytes 1048576 | tf_op jit(solution)/shard_map/psum | solution.py:15
  100.3 417.3 %all-reduce.13.cloned.1.call-start = ((), (), s32[]{:S(2)}) async-start(), calls=%async_computation.3 | async-start | bytes 1048576 | tf_op jit(solution)/shard_map/psum | solution.py:124
  449.7 34.4 %copy-start.1 = (f32[32,4096]{1,0:T(8,128)S(1)}, f32[32,4096]{1,0:T(8,128)}, u32[]{:S(2)}) copy-start(f32[32,4096]{1,0:T(8,128)} %all-reduce.9.cloned.1.call-done) | copy-start | bytes 1572868
  484.8 199.6 %all-reduce.11.cloned.1.call-start = ((), (), s32[]{:S(2)}) async-start(), calls=%async_computation.2 | async-start | bytes 1048576 | tf_op jit(solution)/shard_map/psum | solution.py:142
  587.8 23.7 %copy-start.2 = (f32[32,2048]{1,0:T(8,128)S(1)}, f32[32,2048]{1,0:T(8,128)}, u32[]{:S(2)}) copy-start(f32[32,2048]{1,0:T(8,128)} %get-tuple-element.525) | copy-start | bytes 786436
Sparse Core Ops, SparseCore 0:
  15.4 54.0 all-reduce.6
  100.5 72.7 all-reduce.8
  484.9 32.6 all-reduce.12
  611.6 72.7 all-reduce.10
where the time goes:
time: 741 us; the launch traced here: 738 us
  matrix products  268 us (36%)
  waiting for transfers between devices  231 us (31%)
  other arithmetic  111 us (15%)
  loops' own time  90.1 us (12%)
  blocking collectives  20.6 us (3%)
  between operations  14.1 us (2%)
    psum x2, waiting for transfers between devices, spread_2(): return lax.psum(kept, axis)  126 us
    psum x1, waiting for transfers between devices, body(): sums_cols = lax.psum(jnp.dot(vecs_rows, grown, precision=HIGH), 'row')  72.5 us
    another operation x1, loops' own time, householder(): return lax.fori_loop(0, breadth, reflect_step, start)  65.2 us
    dot_general x64, matrix products, row_step(): lower_row = jnp.dot(picked, lower, precision=HIGH)  49.5 us
    div x64, other arithmetic, row_step(): (rhs_row - jnp.dot(lower_row, solved, precision=HIGH)) / diag_value  40.2 us
    dot_general x1, matrix products, body(): lax.dot_general(vecs_cols, grown, (((1,), (1,)), ((), ())), precision=HIGH)  34.4 us
    dot_general x1, matrix products, body(): lax.dot_general(left_side, right_side, (((0,), (0,)), ((), ())), precisio...  32.9 us
    psum x1, waiting for transfers between devices, body(): lax.psum((partial_cov, partial_top, own_rows), 'col')  32.5 us
  transfers between devices with their start and end apart: 4, of which 4 were waited for; matrix products, arithmetic and copies ran while one was open for 0% of the time, Pallas kernels for 0%

commit v1 on v0

v1 whole, which is shorter than its diff:
```python
import functools

import jax
import jax.numpy as jnp
from jax import lax
from jax.experimental import pallas as pl
from jax.experimental.pallas import tpu as pltpu
from jax.sharding import PartitionSpec as P

B = 32
M = 512
F32 = jnp.float32
BF16 = jnp.bfloat16
HIGH = lax.Precision.HIGHEST
NN = (((1,), (0,)), ((), ()))
NT = (((1,), (1,)), ((), ()))
TN = (((0,), (0,)), ((), ()))


def split(value):
    high = value.astype(BF16)
    return high, (value - high.astype(F32)).astype(BF16)


def split_3(value):
    high = value.astype(BF16)
    rest = value - high.astype(F32)
    middle = rest.astype(BF16)
    return high, middle, (rest - middle.astype(F32)).astype(BF16)


def dot_3(a, b):
    ah, am, al = split_3(a)
    bh, bm, bl = split_3(b)
    return lax.dot_general(
        jnp.concatenate([ah, ah, am, ah, am, al], axis=0),
        jnp.concatenate([bh, bm, bh, bl, bm, bh], axis=0),
        TN,
        preferred_element_type=F32,
    )


def fold(value, count):
    total = value[:B]
    for k in range(1, count):
        total = total + value[k * B : (k + 1) * B]
    return total


ROOM = 30 * 2**20


def room(**more):
    return pltpu.CompilerParams(vmem_limit_bytes=ROOM, **more)


def whole(shape):
    return pl.BlockSpec(shape, lambda i, *place: (0,) * len(shape))


def standardize(dosage, freq, individuals=1):
    allele = freq.astype(F32) / 10000.0
    spread = jnp.sqrt(2.0 * allele * (1.0 - allele))
    allele, spread = (jnp.expand_dims(value, individuals) for value in (allele, spread))
    scaled = (dosage.astype(F32) / 100.0 - 2.0 * allele) / spread
    return scaled.astype(BF16)


def strip_kernel(place_ref, source_ref, strip_ref, turned_ref):
    turned_ref[...] = source_ref[...].astype(F32).T
    strip_ref[...] = turned_ref[pl.ds(pl.multiple_of(place_ref[1], B), B), :]


def take_strip(source, offset):
    rows = source.shape[0]
    width = min(128, source.shape[1])
    place = jnp.stack([offset // width, offset % width]).astype(jnp.int32)
    return pl.pallas_call(
        strip_kernel,
        out_shape=jax.ShapeDtypeStruct((B, rows), F32),
        grid_spec=pltpu.PrefetchScalarGridSpec(
            num_scalar_prefetch=1,
            grid=(1,),
            in_specs=[pl.BlockSpec((rows, width), lambda i, place: (0, place[0]))],
            out_specs=pl.BlockSpec((B, rows), lambda i, place: (0, 0)),
            scratch_shapes=[pltpu.VMEM((width, rows), F32)],
        ),
        compiler_params=room(),
        name="strip",
    )(place, source)


def lifted(strip, ids, factor, lift):
    slots = lax.broadcasted_iota(jnp.int32, (B, 1), 0)
    select = jnp.where(ids == slots, 1.0, 0.0).astype(BF16)
    taken = lax.dot_general(
        jnp.concatenate(split_3(factor), axis=0),
        jnp.concatenate([select] * 3, axis=0),
        TN,
        preferred_element_type=F32,
    )
    return dot_3(lift, jnp.where(ids >= 0, strip, 0.0) - taken)


def lane_ids(width, start):
    return start + lax.broadcasted_iota(jnp.int32, (1, width), 1)


def panel_kernel(place_ref, raw_ref, chosen_ref, scaled_ref, strip_ref, small_ref):
    strip = raw_ref[...] + jnp.dot(
        chosen_ref[...], scaled_ref[...], preferred_element_type=F32
    ) * (1.0 / M)
    strip_ref[...] = strip
    ids = lane_ids(strip.shape[1], place_ref[0])
    slots = lax.broadcasted_iota(jnp.int32, (B, 1), 0)
    select = jnp.where(ids == slots, 1.0, 0.0).astype(BF16)
    parts = jnp.concatenate(split_3(strip), axis=0)
    rest = jnp.where(ids >= B, parts, jnp.zeros_like(parts))
    square = lax.dot_general(
        jnp.concatenate([select, rest], axis=0), parts, NT, preferred_element_type=F32
    )
    square = square[:, :B] + square[:, B : 2 * B] + square[:, 2 * B :]
    small_ref[:B, :] = square[:B]
    small_ref[B:, :] = fold(square[B:], 3)


def panel_block(place, raw, chosen, scaled):
    width = raw.shape[1]
    return pl.pallas_call(
        panel_kernel,
        out_shape=(
            jax.ShapeDtypeStruct((B, width), F32),
            jax.ShapeDtypeStruct((2 * B, B), F32),
        ),
        grid_spec=pltpu.PrefetchScalarGridSpec(
            num_scalar_prefetch=1,
            grid=(1,),
            in_specs=[whole(raw.shape), whole(chosen.shape), whole(scaled.shape)],
            out_specs=(whole((B, width)), whole((2 * B, B))),
        ),
        compiler_params=room(),
        name="panel",
    )(place, raw, chosen, scaled)


def product_kernel(
    place_ref, strip_ref, factor_ref, lift_ref, scaled_ref, relation_ref,
    vecs_ref, sums_ref, marks_ref, columns_ref,
):
    @pl.when(pl.program_id(0) == 0)
    def _():
        width = strip_ref.shape[1]
        ids = lane_ids(width, place_ref[0])
        vecs = lifted(strip_ref[...], ids, factor_ref[...], lift_ref[...])
        vecs_ref[...] = vecs
        high, low = split(vecs)
        both = jnp.concatenate([high, low], axis=0)
        both = jnp.concatenate([both, jnp.zeros_like(both)], axis=0)
        columns_ref[...] = both.astype(F32).T.astype(BF16)
        marks_ref[...] = fold(
            lax.dot_general(both, scaled_ref[...], NT, preferred_element_type=F32), 2
        )

    step = sums_ref.shape[1]
    here = pl.ds(pl.multiple_of(pl.program_id(0) * step, step), step)
    high, low = split(relation_ref[here, :])
    columns = columns_ref[...]
    product = jnp.dot(high, columns, preferred_element_type=F32) + jnp.dot(
        low, columns, preferred_element_type=F32
    )
    sums_ref[...] = fold(product.T, 2)


def tile_product(place, strip, factor, lift, scaled, relation):
    rows, width = relation.shape
    step = min(256, rows)
    return pl.pallas_call(
        product_kernel,
        out_shape=(
            jax.ShapeDtypeStruct((B, width), F32),
            jax.ShapeDtypeStruct((B, rows), F32),
            jax.ShapeDtypeStruct((B, M), F32),
        ),
        grid_spec=pltpu.PrefetchScalarGridSpec(
            num_scalar_prefetch=1,
            grid=(rows // step,),
            in_specs=[
                whole(strip.shape),
                whole((B, B)),
                whole((B, B)),
                whole(scaled.shape),
                pl.BlockSpec(memory_space=pltpu.VMEM),
            ],
            out_specs=(
                whole((B, width)),
                pl.BlockSpec((B, step), lambda i, place: (0, i)),
                whole((B, M)),
            ),
            scratch_shapes=[pltpu.VMEM((width, 4 * B), BF16)],
        ),
        cost_estimate=pl.CostEstimate(
            flops=16 * B * rows * width, bytes_accessed=4 * rows * width, transcendentals=0
        ),
        compiler_params=room(),
        name="product",
    )(place, strip, factor, lift, scaled, relation)


def rows_kernel(
    place_ref, raw_ref, chosen_ref, scaled_ref, factor_ref, lift_ref, sums_ref,
    vecs_ref, inner_ref, turned_ref,
):
    scaled = scaled_ref[...]
    strip = raw_ref[...] + jnp.dot(
        chosen_ref[...], scaled, preferred_element_type=F32
    ) * (1.0 / M)
    ids = lane_ids(strip.shape[1], place_ref[0])
    vecs = lifted(strip, ids, factor_ref[...], lift_ref[...])
    vecs_ref[...] = vecs
    square = lax.dot_general(
        jnp.concatenate(split(vecs), axis=0),
        jnp.concatenate(split(sums_ref[...]), axis=0),
        NT,
        preferred_element_type=F32,
    )
    inner_ref[...] = fold(square[:, :B] + square[:, B:], 2)
    turned_ref[...] = (scaled.astype(F32) * (1.0 / M)).T.astype(BF16)


def row_block(place, raw, chosen, scaled, factor, lift, sums):
    args = (raw, chosen, scaled, factor, lift, sums)
    outs = ((raw.shape, F32), ((B, B), F32), (scaled.shape[::-1], BF16))
    return pl.pallas_call(
        rows_kernel,
        out_shape=tuple(jax.ShapeDtypeStruct(*out) for out in outs),
        grid_spec=pltpu.PrefetchScalarGridSpec(
            num_scalar_prefetch=1,
            grid=(1,),
            in_specs=[whole(a.shape) for a in args],
            out_specs=tuple(whole(out[0]) for out in outs),
        ),
        compiler_params=room(),
        name="rows",
    )(place, *args)


def reflect_kernel(small_ref, factor_ref, lift_ref, triangle_ref):
    rows = lax.broadcasted_iota(jnp.int32, (B, B), 0)
    lanes = lax.broadcasted_iota(jnp.int32, (B, B), 1)
    row = lax.broadcasted_iota(jnp.int32, (B, 1), 0)
    lane = lax.broadcasted_iota(jnp.int32, (1, B), 1)
    eye = jnp.where(rows == lanes, 1.0, 0.0).astype(F32)
    work = small_ref[:B, :]
    cross = small_ref[B:, :]
    lift = eye
    triangle = jnp.zeros((B, B), F32)
    diagonal = jnp.zeros((1, B), F32)
    for j in range(B):
        column = jnp.where(row >= j, work[:, j : j + 1], 0.0)
        lift_column = lift[:, j : j + 1]
        cross_column = cross[:, j : j + 1]
        inner = jnp.sum(column * work, axis=0, keepdims=True) + jnp.sum(
            lift_column * cross, axis=0, keepdims=True
        )
        square = inner[:, j : j + 1]
        alpha = work[j : j + 1, j : j + 1]
        length = jnp.sqrt(square)
        shift = jnp.where(alpha >= 0.0, length, -length)
        tau = 1.0 / (length * (length + jnp.abs(alpha)))
        inner = inner + shift * work[j : j + 1, :]
        vector = column + jnp.where(row == j, shift, 0.0)
        kappa = jnp.where(lane > j, tau * inner, 0.0)
        work = work - vector * kappa
        work = work + jnp.where((rows == j) & (lanes == j), shift, 0.0)
        lift = lift - lift_column * kappa
        cross = cross - cross_column * kappa
        past = jnp.sum(triangle * jnp.where(lane < j, inner, 0.0), axis=1, keepdims=True)
        new = tau * (jnp.where(row == j, 1.0, 0.0) - past)
        triangle = jnp.where(lanes == j, new, triangle)
        diagonal = jnp.where(lane == j, -shift, diagonal)
    factor_ref[...] = jnp.where(rows < lanes, work, 0.0) + jnp.where(rows == lanes, diagonal, 0.0)
    lift_ref[...] = lift
    triangle_ref[...] = triangle


def reflect(small):
    out = jax.ShapeDtypeStruct((B, B), F32)
    return pl.pallas_call(
        reflect_kernel, out_shape=(out,) * 3, compiler_params=room(), name="reflect"
    )(small)


def update_kernel(
    triangle_ref, inner_ref, marks_ref, turned_ref, scaled_rows_ref, vecs_rows_ref,
    sums_rows_ref, scaled_cols_ref, vecs_cols_ref, sums_cols_ref, relation_ref,
    out_ref, left_ref, half_ref,
):
    def dot(a, b, dims):
        return lax.dot_general(a, b, dims, precision=HIGH, preferred_element_type=F32)

    def parts(vecs, sums, scaled):
        marks = jnp.concatenate(split(marks_ref[...] * (1.0 / M)), axis=0)
        full = sums + fold(
            lax.dot_general(marks, scaled, NN, preferred_element_type=F32), 2
        )
        th, tl = split(triangle_ref[...])
        hh, hl = split(-half_ref[...])
        fh, fl = split(full)
        vh, vl = split(vecs)
        adjusted = lax.dot_general(
            jnp.concatenate([th, th, tl, hh, hh, hl], axis=0),
            jnp.concatenate([fh, fl, fh, vh, vl, vh], axis=0),
            TN,
            preferred_element_type=F32,
        )
        return (vh, vl) + split(adjusted)

    @pl.when(pl.program_id(0) == 0)
    def _():
        triangle = triangle_ref[...]
        marks = marks_ref[...]
        inner = inner_ref[...] + dot(marks, marks, NT) * (1.0 / M)
        half_ref[...] = 0.5 * dot(triangle, dot(inner, triangle, NN), TN)
        vh, vl, ah, al = parts(
            vecs_rows_ref[...], sums_rows_ref[...], scaled_rows_ref[...]
        )
        left = jnp.concatenate([vh, vh, vl, vl, ah, ah, al, al], axis=0)
        left_ref[...] = left.astype(F32).T.astype(BF16)

    scaled = scaled_cols_ref[...]
    vh, vl, ah, al = parts(vecs_cols_ref[...], sums_cols_ref[...], scaled)
    right = -jnp.concatenate([ah, al, ah, al, vh, vl, vh, vl], axis=0)
    rows, step = out_ref.shape
    here = pl.ds(pl.multiple_of(pl.program_id(0) * step, step), step)
    chunk = min(512, rows)
    for k in range(rows // chunk):
        some = pl.ds(k * chunk, chunk)
        out_ref[some, :] = (
            relation_ref[some, here]
            + jnp.dot(turned_ref[some, :], scaled, preferred_element_type=F32)
            + jnp.dot(left_ref[some, :], right, preferred_element_type=F32)
        )


def tile_update(triangle, inner, marks, of_rows, of_cols, relation):
    rows, width = relation.shape
    step = min(512, width)

    def full(value):
        return pl.BlockSpec(value.shape, lambda i: (0, 0), pipeline_mode=pl.Buffered(1))

    def slab(value):
        return pl.BlockSpec((value.shape[0], step), lambda i: (0, i))

    fixed = (triangle, inner, marks) + of_rows
    return pl.pallas_call(
        update_kernel,
        out_shape=jax.ShapeDtypeStruct((rows, width), F32),
        grid=(width // step,),
        in_specs=[full(value) for value in fixed]
        + [slab(value) for value in of_cols]
        + [pl.BlockSpec(memory_space=pltpu.VMEM)],
        out_specs=slab(relation),
        scratch_shapes=[pltpu.VMEM((rows, 8 * B), BF16), pltpu.VMEM((B, B), F32)],
        cost_estimate=pl.CostEstimate(
            flops=2 * (M + 8 * B) * rows * width,
            bytes_accessed=8 * rows * width,
            transcendentals=0,
        ),
        compiler_params=room(),
        name="update",
    )(*fixed, *of_cols, relation)


def swap(value, axis, size, bit):
    return lax.ppermute(value, axis, [(i, i ^ bit) for i in range(size)])


def bits_of(size):
    return [1 << b for b in range(size.bit_length() - 1)]


def make_body(n_row, n_col):
    per = n_row // n_col
    both = ("row", "col")

    def body(relation, dosage, freq, panel):
        tile_rows, tile_cols = relation.shape
        row_id = lax.axis_index("row")
        col_id = lax.axis_index("col")
        place = panel[0]
        first_row = (place + 1) * B
        panel_col = place * B // tile_cols
        panel_off = place * B % tile_cols
        own_col = row_id // per

        def from_panel(value, bits):
            for bit in bits:
                other = swap(value, "col", n_col, bit)
                value = jnp.where(((col_id ^ panel_col) & bit) != 0, other, value)
            return value

        def to_column(block):
            total = jnp.where(own_col == col_id, block, 0.0)
            received = []
            for shift in range(1, n_col):
                pairs = []
                for c in range(n_col):
                    for s in range(per):
                        source = (c * per + s) * n_col + c
                        target = (((c + shift) % n_col) * per + s) * n_col + c
                        pairs.append((source, target))
                received.append(lax.ppermute(block, both, pairs))
            for other in received:
                total = total + other
            return total

        def join_column(block):
            mine = row_id % per
            parts = [None] * per
            got = [block]
            for shift in range(1, per):
                pairs = [
                    (r, (r // per) * per + (r % per) ^ shift) for r in range(n_row)
                ]
                got.append(lax.ppermute(block, "row", pairs))
            for s in range(per):
                value = got[0]
                for shift in range(1, per):
                    value = jnp.where((mine ^ s) == shift, got[shift], value)
                parts[s] = value
            return jnp.concatenate(parts, axis=1)

        raw_rows = take_strip(relation, panel_off)
        held = pltpu.with_memory_space_constraint(relation, pltpu.VMEM)
        raw_rows = from_panel(raw_rows, [1])
        dosage, raw_rows = lax.optimization_barrier((dosage, raw_rows))
        scaled = standardize(dosage, freq)
        chosen = take_strip(dosage, panel_off)
        chosen = from_panel(standardize(chosen, freq, 0), bits_of(n_col))
        raw_rows = from_panel(raw_rows, bits_of(n_col)[1:])

        own = lax.dynamic_slice_in_dim(scaled, (row_id % per) * tile_rows, tile_rows, 1)

        def spread_rows(value, bit):
            pairs = []
            for r in range(n_row):
                for c in range(n_col):
                    apart = c ^ (r // per)
                    if bit == 1:
                        if apart == 0:
                            pairs.append((r * n_col + c, r * n_col + (c ^ 1)))
                    elif (apart & ~1) & ~(bit - 1) == 0:
                        pairs.append((r * n_col + c, r * n_col + (c ^ bit)))
            other = lax.ppermute(value, both, pairs)
            apart = col_id ^ own_col
            if bit == 1:
                take = (apart & 1) != 0
            else:
                take = (apart & bit) != 0
            return jnp.where(take, other, value)

        own = spread_rows(own, 1)
        core = col_id % 2
        half = M // 2
        part = lax.dynamic_slice_in_dim(own, core * half, half, 0)
        part, raw_rows = lax.optimization_barrier((part, raw_rows))
        for bit in bits_of(n_col)[1:]:
            part = spread_rows(part, bit)
        other = swap(part, "col", n_col, 1)
        rows_scaled = jnp.concatenate(
            [jnp.where(core == 0, part, other), jnp.where(core == 0, other, part)], axis=0
        )

        raw_cols = join_column(to_column(raw_rows))
        place_cols = jnp.reshape(col_id * tile_cols - first_row, (1,)).astype(jnp.int32)
        place_rows = jnp.reshape(row_id * tile_rows - first_row, (1,)).astype(jnp.int32)
        strip_cols, small = panel_block(place_cols, raw_cols, chosen, scaled)
        for bit in bits_of(n_col):
            small = small + swap(small, "col", n_col, bit)
        small, rows_scaled = lax.optimization_barrier((small, rows_scaled))
        factor, lift, triangle = reflect(small)

        vecs_cols, part_sums, part_marks = tile_product(
            place_cols, strip_cols, factor, lift, scaled, held
        )
        sums = jnp.concatenate([part_sums, part_marks], axis=1)
        width = sums.shape[1] // 2
        kept = lax.dynamic_slice_in_dim(sums, core * width, width, 1)
        sent = lax.dynamic_slice_in_dim(sums, (1 - core) * width, width, 1)
        vecs_rows, inner, turned = row_block(
            place_rows, raw_rows, chosen, rows_scaled, factor, lift, part_sums
        )
        kept = kept + swap(sent, "col", n_col, 1)
        inner = inner + swap(inner, "col", n_col, 1)
        for bit in bits_of(n_col)[1:]:
            other = swap(kept, "col", n_col, bit)
            other, inner = lax.optimization_barrier((other, inner))
            kept = kept + other
            inner = inner + swap(inner, "col", n_col, bit)
        other = swap(kept, "col", n_col, 1)
        sums = jnp.concatenate(
            [jnp.where(core == 0, kept, other), jnp.where(core == 0, other, kept)], axis=1
        )
        sums_rows, marks = sums[:, :tile_rows], sums[:, tile_rows:]
        for bit in bits_of(n_row):
            inner = inner + swap(inner, "row", n_row, bit)
        sums_cols = join_column(to_column(sums_rows))
        return tile_update(
            triangle,
            inner,
            marks,
            (turned, rows_scaled, vecs_rows, sums_rows),
            (scaled, vecs_cols, sums_cols),
            held,
        )

    return body


def solution(mesh):
    placed = (P("row", "col"), P(None, "col"), P(), P())
    body = make_body(mesh.shape["row"], mesh.shape["col"])
    return jax.shard_map(
        body, mesh=mesh, in_specs=placed, out_specs=P("row", "col"), check_vma=False
    )
```

time: 741 us -> 182 us (0.25)
  matrix products: 268 us -> 0 us
  waiting for transfers between devices: 231 us -> 45.8 us
  other arithmetic: 111 us -> 10.2 us
  loops' own time: 90.1 us -> 0 us
  Pallas kernels: 0 us -> 50.5 us
  starting transfers between devices: 0.35 us -> 38.6 us
  local copies, waits for them, and re-layouts: 2 us -> 35.5 us
  blocking collectives: 20.6 us -> 0 us
  between operations: 14.1 us -> 1.07 us
    dot_general x400 -> x0, matrix products: 268 us -> none  [the longest x64 49.5 us: row_step(): lower_row = jnp.dot(picked, lower, precision=HIGH)]
    psum x4 -> x0, waiting for transfers between devices: 231 us -> none  [the longest x2 126 us: spread_2(): return lax.psum(kept, axis)]
    another operation x4 -> x0, loops' own time: 90.1 us -> none  [the longest x1 65.2 us: householder(): return lax.fori_loop(0, breadth, reflect_step, start)]
    pallas_call x0 -> x7, Pallas kernels: none -> 50.5 us  [the longest x1 22.4 us: tile_update(): pl.pallas_call(update_kernel, out_shape=jax.ShapeDtypeStruct((rows, width...]
    ppermute x0 -> x25, waiting for transfers between devices: none -> 45.8 us  [the longest x15 29.1 us: swap(): return lax.ppermute(value, axis, [(i, i ^ bit) for i in range(size)])]
    reduce_sum x96 -> x0, other arithmetic: 45.3 us -> none  [the longest x32 21.8 us: reflect_step(): length = jnp.sqrt(jnp.sum(below * below))]
    div x64 -> x0, other arithmetic: 40.2 us -> none  [row_step(): (rhs_row - jnp.dot(lower_row, solved, precision=HIGH)) / diag_value]
    ppermute x0 -> x25, starting transfers between devices: none -> 38.6 us  [the longest x15 14.8 us: swap(): return lax.ppermute(value, axis, [(i, i ^ bit) for i in range(size)])]
  transfers between devices with their start and end apart: 4 -> 25, of which waited for: 4 -> 20; matrix products, arithmetic and copies ran while one was open for 0% -> 1% of each run, Pallas kernels for 0% -> 2%
where the time goes in v1:
time: 182 us
  Pallas kernels  50.5 us (28%)
  waiting for transfers between devices  45.8 us (25%)
  starting transfers between devices  38.6 us (21%)
  local copies, waits for them, and re-layouts  35.5 us (20%)
  other arithmetic  10.2 us (6%)
    unnamed x35, local copies, waits for them, and re-layouts  32.5 us
    ppermute x15, waiting for transfers between devices, swap(): return lax.ppermute(value, axis, [(i, i ^ bit) for i in range(size)])  29.1 us
    pallas_call x1, Pallas kernels, tile_update(): pl.pallas_call(update_kernel, out_shape=jax.ShapeDtypeStruct((rows, width...  22.4 us
    pallas_call x1, Pallas kernels, tile_product(): pl.pallas_call(product_kernel, out_shape=(jax.ShapeDtypeStruct((B, width)...  15.6 us
    ppermute x15, starting transfers between devices, swap(): return lax.ppermute(value, axis, [(i, i ^ bit) for i in range(size)])  14.8 us
    ppermute x6, starting transfers between devices, to_column(): received.append(lax.ppermute(block, both, pairs))  12.4 us
    ppermute x6, waiting for transfers between devices, to_column(): received.append(lax.ppermute(block, both, pairs))  12.2 us
    ppermute x2, starting transfers between devices, spread_rows(): other = lax.ppermute(value, both, pairs)  8.28 us
  transfers between devices with their start and end apart: 25, of which 20 were waited for; matrix products, arithmetic and copies ran while one was open for 1% of the time, Pallas kernels for 2%

profile of v1, /device:TPU:0, one launch (start us, length us, event | category | flops | bytes accessed | tf_op | source)
XLA Modules:
  0.0 181.6 jit_solution(841381153531843058)
XLA Ops:
  0.8 2.1 %strip.2 = f32[32,2048]{1,0:T(8,128)S(1)} custom-call(s32[2]{0:T(128)S(1)} %pad_add_fusion.place_ref, f32[2048,4096]{1,0:T(8,128)} %relation_ref.3), custom_call_target="tpu_custom_call" | custom-call | tf_op jit(solution)/shard_map/strip/pallas_call | solution.py:78
  2.9 0.6 collective-permute-start
  3.5 1.1 collective-permute-done
  4.7 4.4 %divide_convert_fusion.scaled_ref.scaled_cols_ref = bf16[512,4096]{1,0:T(8,128)(2,1)S(1)} fusion(s32[512,4096]{1,0:T(8,128)} %source_ref.2, f32[512]{0:T(512)S(1)} %get-tuple-element.52, f32[512]{0:T(512)S(1)} %get-tuple-element.51), kind=kLoop, calls=%fused_computation | loop fusion | flops 10485760 | bytes 12587008 | tf_op jit(solution)/shard_map/convert_element_type | solution.py:66
  9.0 1.9 %copy-done.2 = bf16[512,4096]{1,0:T(8,128)(2,1)} copy-done((bf16[512,4096]{1,0:T(8,128)(2,1)}, bf16[512,4096]{1,0:T(8,128)(2,1)S(1)}, u32[]{:S(2)}) %copy-start.2) | copy-done | bytes 4194328
  11.0 1.5 constant_dynamic-slice_fusion.1
  12.4 3.6 %collective-permute-start.1 = (bf16[512,2048]{1,0:T(8,128)(2,1)}, bf16[512,2048]{1,0:T(8,128)(2,1)}, u32[]{:S(2)}, u32[]{:S(2)}) collective-permute-start(bf16[512,2048]{1,0:T(8,128)(2,1)} %constant_dynamic-slice_fusion.1), channel_id=1, source_target_pairs={{0,1},{4,5},{9,8},{13,12},{18,19},{22,23},{27,26},{31,30}} | collective-permute-start | bytes 6291464 | tf_op jit(solution)/shard_map/ppermute | solution.py:455
  16.1 1.2 collective-permute-start.2
  17.3 6.6 %collective-permute-done.2 = f32[32,2048]{1,0:T(8,128)S(1)} collective-permute-done((f32[32,2048]{1,0:T(8,128)S(1)}, f32[32,2048]{1,0:T(8,128)S(1)}, u32[]{:S(2)}, u32[]{:S(2)}) %collective-permute-start.2) | collective-permute-done | bytes 262176 | tf_op jit(solution)/shard_map/ppermute | solution.py:376
  24.0 1.9 %dynamic-slice_select_fusion = bf16[256,2048]{1,0:T(8,128)(2,1)S(1)} fusion(bf16[512,4096]{1,0:T(8,128)(2,1)} %copy-done.2, s32[]{:T(128)S(6)} %select_n.160, s32[]{:T(128)S(6)} %select_n.157, bf16[512,2048]{1,0:T(8,128)(2,1)} %collective-permute-done.1, pred[]{:T(512)S(6)} %ne.56), kind=kLoop, calls=%fused_computation.2 | loop fusion | flops 524288 | bytes 3145737 | tf_op jit(solution)/shard_map/jit(_where)/select_n | solution.py:461
  25.9 4.7 %collective-permute-start.11 = (bf16[256,2048]{1,0:T(8,128)(2,1)S(1)}, bf16[256,2048]{1,0:T(8,128)(2,1)}, u32[]{:S(2)}, u32[]{:S(2)}) collective-permute-start(bf16[256,2048]{1,0:T(8,128)(2,1)S(1)} %dynamic-slice_select_fusion), channel_id=1, source_target_pairs={{0,2},{1,3},{4,6},{5,7},{8,10},{9,11},{12,14},{13,15},{18,16},{19,... | collective-permute-start | bytes 3145736 | tf_op jit(solution)/shard_map/ppermute | solution.py:455
  30.6 3.4 %copy-done.4 = s32[512,4096]{1,0:T(8,128)S(1)} copy-done((s32[512,4096]{1,0:T(8,128)S(1)}, s32[512,4096]{1,0:T(8,128)}, u32[]{:S(2)}) %copy-start.4) | copy-done | bytes 8388632
  33.9 0.7 strip.3
  34.6 2.7 %collective-permute-start.5 = (f32[32,2048]{1,0:T(8,128)S(1)}, f32[32,2048]{1,0:T(8,128)S(1)}, u32[]{:S(2)}, u32[]{:S(2)}) collective-permute-start(f32[32,2048]{1,0:T(8,128)S(1)} %broadcast_select_fusion.5.raw_ref), channel_id=1, source_target_pairs={{0,24},{4,28},{9,1},{13,5},{18,10},{22,14},{27,19},{31,23}} | collective-permute-start | bytes 786440 | tf_op jit(solution)/shard_map/ppermute | solution.py:413
  37.4 1.3 collective-permute-start.4
  38.7 1.3 collective-permute-start.3
  40.1 1.2 collective-permute-done.7
  41.4 2.7 %collective-permute-done.4 = f32[32,2048]{1,0:T(8,128)S(1)} collective-permute-done((f32[32,2048]{1,0:T(8,128)S(1)}, f32[32,2048]{1,0:T(8,128)S(1)}, u32[]{:S(2)}, u32[]{:S(2)}) %collective-permute-start.4) | collective-permute-done | bytes 262176 | tf_op jit(solution)/shard_map/ppermute | solution.py:413
  44.1 2.8 %collective-permute-done.3 = f32[32,2048]{1,0:T(8,128)S(1)} collective-permute-done((f32[32,2048]{1,0:T(8,128)S(1)}, f32[32,2048]{1,0:T(8,128)S(1)}, u32[]{:S(2)}, u32[]{:S(2)}) %collective-permute-start.3) | collective-permute-done | bytes 262176 | tf_op jit(solution)/shard_map/ppermute | solution.py:413
  46.9 1.6 collective-permute-start.6
  48.5 3.2 %collective-permute-done.11 = bf16[256,2048]{1,0:T(8,128)(2,1)} collective-permute-done((bf16[256,2048]{1,0:T(8,128)(2,1)S(1)}, bf16[256,2048]{1,0:T(8,128)(2,1)}, u32[]{:S(2)}, u32[]{:S(2)}) %collective-permute-start.11) | collective-permute-done | bytes 1048608 | tf_op jit(solution)/shard_map/ppermute | solution.py:455
  52.0 0.2 collective-permute-done.8
  52.1 1.3 collective-permute-done.6
  53.5 1.3 panel.1
  54.8 0.8 copy-done.8
  55.6 1.2 collective-permute-done.9
  56.8 4.9 %collective-permute-start.10 = (f32[64,32]{1,0:T(8,128)S(1)}, f32[64,32]{1,0:T(8,128)S(1)}, u32[]{:S(2)}, u32[]{:S(2)}) collective-permute-start(f32[64,32]{1,0:T(8,128)S(1)} %add.90), channel_id=1, source_target_pairs={{0,2},{1,3},{2,0},{3,1},{4,6},{5,7},{6,4},{7,5},{8,10},{9,11},{10,... | collective-permute-start | bytes 24584 | tf_op jit(solution)/shard_map/ppermute | solution.py:376
  61.7 1.9 %collective-permute-done.10 = f32[64,32]{1,0:T(8,128)S(1)} collective-permute-done((f32[64,32]{1,0:T(8,128)S(1)}, f32[64,32]{1,0:T(8,128)S(1)}, u32[]{:S(2)}, u32[]{:S(2)}) %collective-permute-start.10) | collective-permute-done | bytes 8224 | tf_op jit(solution)/shard_map/ppermute | solution.py:376
  63.8 1.6 pad_maximum_fusion.scaled_ref.scaled_rows_ref
  65.4 7.1 %reflect.1 = (f32[32,32]{1,0:T(8,128)S(1)}, f32[32,32]{1,0:T(8,128)S(1)}, f32[32,32]{1,0:T(8,128)S(1)}) custom-call(f32[64,32]{1,0:T(8,128)S(1)} %add.91.small_ref), custom_call_target="tpu_custom_call" | custom-call | tf_op jit(solution)/shard_map/reflect/pallas_call | solution.py:288
  72.5 0.6 copy-done.10
  73.1 0.6 copy-done.12
  73.7 0.6 copy-done.14
  74.3 10.5 %copy-done = f32[2048,4096]{1,0:T(8,128)S(1)} copy-done((f32[2048,4096]{1,0:T(8,128)S(1)}, f32[2048,4096]{1,0:T(8,128)}, u32[]{:S(2)}) %copy-start) | copy-done | bytes 33554456
  84.9 15.6 %product.1 = (f32[32,4096]{1,0:T(8,128)}, f32[32,2048]{1,0:T(8,128)}, f32[32,512]{1,0:T(8,128)}) custom-call(s32[1]{0:T(128)} %bitcast.1.place_ref, f32[32,4096]{1,0:T(8,128)} %copy-done.8, f32[32,32]{1,0:T(8,128)} %copy-done.10, f32[32,32]{1,0:T(8,128)} %copy-done.12, bf16[512,4096]{1,0:T(8,128)(2,1)} %copy-done.2, f32[2048,4096]{1,0:T(8,128)S(1)} %copy-done), custom_call_target="tpu_custom_call" | custom-call | flops 4294967296 | bytes 33554432 | tf_op jit(solution)/shard_map/product/pallas_call | solution.py:177
  100.5 1.0 constant_dynamic-update-slice_fusion.1
  101.5 0.8 constant_dynamic-update-slice_fusion
  102.4 1.4 collective-permute-done.13
  103.8 2.1 %collective-permute-start.14 = (f32[32,1280]{1,0:T(8,128)S(1)}, f32[32,1280]{1,0:T(8,128)S(1)}, u32[]{:S(2)}, u32[]{:S(2)}) collective-permute-start(f32[32,1280]{1,0:T(8,128)S(1)} %dynamic-slice_add_fusion), channel_id=1, source_target_pairs={{0,2},{1,3},{2,0},{3,1},{4,6},{5,7},{6,4},{7,5},{8,10},{9,11},{10,... | collective-permute-start | bytes 491528 | tf_op jit(solution)/shard_map/ppermute | solution.py:376
  105.9 1.6 copy-done.5
  107.5 0.9 copy-done.7
  108.5 1.2 rows.1
  109.8 1.2 collective-permute-done.15
  111.0 0.2 collective-permute-start.20
  111.2 1.2 collective-permute-done.20
  112.5 4.2 %collective-permute-start.23 = (f32[32,2048]{1,0:T(8,128)S(1)}, f32[32,2048]{1,0:T(8,128)S(1)}, u32[]{:S(2)}, u32[]{:S(2)}) collective-permute-start(f32[32,2048]{1,0:T(8,128)S(1)} %pad_maximum_fusion.3.sums_rows_ref), channel_id=1, source_target_pairs={{0,24},{4,28},{9,1},{13,5},{18,10},{22,14},{27,19},{31,23}} | collective-permute-start | bytes 786440 | tf_op jit(solution)/shard_map/ppermute | solution.py:413
  116.8 1.3 collective-permute-start.22
  118.1 1.5 collective-permute-start.21
  119.6 1.1 collective-permute-done.23
  120.7 2.8 %collective-permute-done.22 = f32[32,2048]{1,0:T(8,128)S(1)} collective-permute-done((f32[32,2048]{1,0:T(8,128)S(1)}, f32[32,2048]{1,0:T(8,128)S(1)}, u32[]{:S(2)}, u32[]{:S(2)}) %collective-permute-start.22) | collective-permute-done | bytes 262176 | tf_op jit(solution)/shard_map/ppermute | solution.py:413
  123.5 2.8 %collective-permute-done.21 = f32[32,2048]{1,0:T(8,128)S(1)} collective-permute-done((f32[32,2048]{1,0:T(8,128)S(1)}, f32[32,2048]{1,0:T(8,128)S(1)}, u32[]{:S(2)}, u32[]{:S(2)}) %collective-permute-start.21) | collective-permute-done | bytes 262176 | tf_op jit(solution)/shard_map/ppermute | solution.py:413
  126.3 1.6 collective-permute-start.24
  127.9 4.7 %collective-permute-start.16 = (f32[32,32]{1,0:T(8,128)S(1)}, f32[32,32]{1,0:T(8,128)S(1)}, u32[]{:S(2)}, u32[]{:S(2)}) collective-permute-start(f32[32,32]{1,0:T(8,128)S(1)} %add.95), channel_id=1, source_target_pairs={{0,2},{1,3},{2,0},{3,1},{4,6},{5,7},{6,4},{7,5},{8,10},{9,11},{10,... | collective-permute-start | bytes 12296 | tf_op jit(solution)/shard_map/ppermute | solution.py:376
  132.6 1.7 collective-permute-done.16
  134.4 0.5 collective-permute-start.17
  134.9 3.2 %collective-permute-done.17 = f32[32,32]{1,0:T(8,128)S(1)} collective-permute-done((f32[32,32]{1,0:T(8,128)S(1)}, f32[32,32]{1,0:T(8,128)S(1)}, u32[]{:S(2)}, u32[]{:S(2)}) %collective-permute-start.17) | collective-permute-done | bytes 4128 | tf_op jit(solution)/shard_map/ppermute | solution.py:376
  138.1 0.2 collective-permute-start.18
  138.3 3.5 %collective-permute-done.18 = f32[32,32]{1,0:T(8,128)S(1)} collective-permute-done((f32[32,32]{1,0:T(8,128)S(1)}, f32[32,32]{1,0:T(8,128)S(1)}, u32[]{:S(2)}, u32[]{:S(2)}) %collective-permute-start.18) | collective-permute-done | bytes 4128 | tf_op jit(solution)/shard_map/ppermute | solution.py:376
  141.8 4.6 %collective-permute-done.19 = f32[32,32]{1,0:T(8,128)S(1)} collective-permute-done((f32[32,32]{1,0:T(8,128)S(1)}, f32[32,32]{1,0:T(8,128)S(1)}, u32[]{:S(2)}, u32[]{:S(2)}) %collective-permute-start.19) | collective-permute-done | bytes 4128 | tf_op jit(solution)/shard_map/ppermute | solution.py:376
  146.5 0.6 add.99.inner_ref
  147.1 0.6 slice.8.marks_ref
  147.8 0.8 pad_maximum_fusion.2.sums_cols_ref
  148.6 10.5 %copy-done.1 = f32[2048,4096]{1,0:T(8,128)S(1)} copy-done((f32[2048,4096]{1,0:T(8,128)S(1)}, f32[2048,4096]{1,0:T(8,128)}, u32[]{:S(2)}) %copy-start.1) | copy-done | bytes 33554456
  159.2 22.4 %update.1 = f32[2048,4096]{1,0:T(8,128)} custom-call(f32[32,32]{1,0:T(8,128)} %copy-done.14, f32[32,32]{1,0:T(8,128)} %add.99.inner_ref, f32[32,512]{1,0:T(8,128)} %slice.8.marks_ref, bf16[2048,512]{1,0:T(8,128)(2,1)} %copy-done.6, bf16[512,2048]{1,0:T(8,128)(2,1)} %pad_maximum_fusion.scaled_ref.scaled_rows_ref, f32[32,2048]{1,0:T(8,128)} %copy-done.9, ...), custom_call_target="tpu_custom_call" | custom-call | flops 12884901888 | bytes 67108864 | tf_op jit(solution)/shard_map/update/pallas_call | solution.py:356
  (61 shorter events, 1.2 us)
Async XLA Ops:
  0.8 2.7 %copy-start.16 = (s32[512]{0:T(512)S(1)}, s32[512]{0:T(512)}, u32[]{:S(2)}) copy-start(s32[512]{0:T(512)} %param.6) | copy-start | bytes 6148
  2.9 1.7 collective-permute-start
  9.0 2.0 %copy-start.2 = (bf16[512,4096]{1,0:T(8,128)(2,1)}, bf16[512,4096]{1,0:T(8,128)(2,1)S(1)}, u32[]{:S(2)}) copy-start(bf16[512,4096]{1,0:T(8,128)(2,1)S(1)} %divide_convert_fusion.scaled_ref.scaled_cols_ref) | copy-start | bytes 12582916
  12.4 11.5 %collective-permute-start.1 = (bf16[512,2048]{1,0:T(8,128)(2,1)}, bf16[512,2048]{1,0:T(8,128)(2,1)}, u32[]{:S(2)}, u32[]{:S(2)}) collective-permute-start(bf16[512,2048]{1,0:T(8,128)(2,1)} %constant_dynamic-slice_fusion.1), channel_id=1, source_target_pairs={{0,1},{4,5},{9,8},{13,12},{18,19},{22,23},{27,26},{31,30}} | collective-permute-start | bytes 6291464 | tf_op jit(solution)/shard_map/ppermute | solution.py:455
  16.1 7.8 %collective-permute-start.2 = (f32[32,2048]{1,0:T(8,128)S(1)}, f32[32,2048]{1,0:T(8,128)S(1)}, u32[]{:S(2)}, u32[]{:S(2)}) collective-permute-start(f32[32,2048]{1,0:T(8,128)S(1)} %broadcast_select_fusion.6), channel_id=1, source_target_pairs={{0,2},{1,3},{2,0},{3,1},{4,6},{5,7},{6,4},{7,5},{8,10},{9,11},{10,... | collective-permute-start | bytes 786440 | tf_op jit(solution)/shard_map/ppermute | solution.py:376
  25.9 25.9 %collective-permute-start.11 = (bf16[256,2048]{1,0:T(8,128)(2,1)S(1)}, bf16[256,2048]{1,0:T(8,128)(2,1)}, u32[]{:S(2)}, u32[]{:S(2)}) collective-permute-start(bf16[256,2048]{1,0:T(8,128)(2,1)S(1)} %dynamic-slice_select_fusion), channel_id=1, source_target_pairs={{0,2},{1,3},{4,6},{5,7},{8,10},{9,11},{12,14},{13,15},{18,16},{19,... | collective-permute-start | bytes 3145736 | tf_op jit(solution)/shard_map/ppermute | solution.py:455
  30.6 3.4 %copy-start.4 = (s32[512,4096]{1,0:T(8,128)S(1)}, s32[512,4096]{1,0:T(8,128)}, u32[]{:S(2)}) copy-start(s32[512,4096]{1,0:T(8,128)} %source_ref.2) | copy-start | bytes 25165828
  34.6 6.8 %collective-permute-start.5 = (f32[32,2048]{1,0:T(8,128)S(1)}, f32[32,2048]{1,0:T(8,128)S(1)}, u32[]{:S(2)}, u32[]{:S(2)}) collective-permute-start(f32[32,2048]{1,0:T(8,128)S(1)} %broadcast_select_fusion.5.raw_ref), channel_id=1, source_target_pairs={{0,24},{4,28},{9,1},{13,5},{18,10},{22,14},{27,19},{31,23}} | collective-permute-start | bytes 786440 | tf_op jit(solution)/shard_map/ppermute | solution.py:413
  37.4 6.7 %collective-permute-start.4 = (f32[32,2048]{1,0:T(8,128)S(1)}, f32[32,2048]{1,0:T(8,128)S(1)}, u32[]{:S(2)}, u32[]{:S(2)}) collective-permute-start(f32[32,2048]{1,0:T(8,128)S(1)} %broadcast_select_fusion.5.raw_ref), channel_id=1, source_target_pairs={{0,16},{4,20},{9,25},{13,29},{18,2},{22,6},{27,11},{31,15}} | collective-permute-start | bytes 786440 | tf_op jit(solution)/shard_map/ppermute | solution.py:413
  38.7 8.2 %collective-permute-start.3 = (f32[32,2048]{1,0:T(8,128)S(1)}, f32[32,2048]{1,0:T(8,128)S(1)}, u32[]{:S(2)}, u32[]{:S(2)}) collective-permute-start(f32[32,2048]{1,0:T(8,128)S(1)} %broadcast_select_fusion.5.raw_ref), channel_id=1, source_target_pairs={{0,8},{4,12},{9,17},{13,21},{18,26},{22,30},{27,3},{31,7}} | collective-permute-start | bytes 786440 | tf_op jit(solution)/shard_map/ppermute | solution.py:413
  40.0 1.3 collective-permute-start.7
  40.1 13.3 %copy-start.3 = (bf16[512,4096]{1,0:T(8,128)(2,1)S(1)}, bf16[512,4096]{1,0:T(8,128)(2,1)}, u32[]{:S(2)}) copy-start(bf16[512,4096]{1,0:T(8,128)(2,1)} %copy-done.2) | copy-start | bytes 12582916
  41.3 10.8 %collective-permute-start.8 = (bf16[32,512]{1,0:T(8,128)(2,1)S(1)}, bf16[32,512]{1,0:T(8,128)(2,1)S(1)}, u32[]{:S(2)}, u32[]{:S(2)}) collective-permute-start(bf16[32,512]{1,0:T(8,128)(2,1)S(1)} %broadcast_select_fusion.11), channel_id=1, source_target_pairs={{0,2},{1,3},{2,0},{3,1},{4,6},{5,7},{6,4},{7,5},{8,10},{9,11},{10,... | collective-permute-start | bytes 98312 | tf_op jit(solution)/shard_map/ppermute | solution.py:376
  46.9 6.4 %collective-permute-start.6 = (f32[32,2048]{1,0:T(8,128)S(1)}, f32[32,2048]{1,0:T(8,128)S(1)}, u32[]{:S(2)}, u32[]{:S(2)}) collective-permute-start(f32[32,2048]{1,0:T(8,128)S(1)} %add_add_fusion.1), channel_id=1, source_target_pairs={{0,4},{4,0},{8,12},{12,8},{16,20},{20,16},{24,28},{28,24},{1,5},{5... | collective-permute-start | bytes 786440 | tf_op jit(solution)/shard_map/ppermute | solution.py:426
  51.9 11.7 %collective-permute-start.12 = (bf16[256,2048]{1,0:T(8,128)(2,1)S(1)}, bf16[256,2048]{1,0:T(8,128)(2,1)S(1)}, u32[]{:S(2)}, u32[]{:S(2)}) collective-permute-start(bf16[256,2048]{1,0:T(8,128)(2,1)S(1)} %broadcast_select_fusion), channel_id=1, source_target_pairs={{0,1},{1,0},{2,3},{3,2},{4,5},{5,4},{6,7},{7,6},{8,9},{9,8},{10,11... | collective-permute-start | bytes 3145736 | tf_op jit(solution)/shard_map/ppermute | solution.py:376
  54.8 0.8 copy-start.8
  55.6 1.2 collective-permute-start.9
  56.8 6.8 %collective-permute-start.10 = (f32[64,32]{1,0:T(8,128)S(1)}, f32[64,32]{1,0:T(8,128)S(1)}, u32[]{:S(2)}, u32[]{:S(2)}) collective-permute-start(f32[64,32]{1,0:T(8,128)S(1)} %add.90), channel_id=1, source_target_pairs={{0,2},{1,3},{2,0},{3,1},{4,6},{5,7},{6,4},{7,5},{8,10},{9,11},{10,... | collective-permute-start | bytes 24584 | tf_op jit(solution)/shard_map/ppermute | solution.py:376
  72.5 0.6 copy-start.10
  73.1 0.6 copy-start.12
  73.7 0.6 copy-start.14
  74.3 10.5 %copy-start = (f32[2048,4096]{1,0:T(8,128)S(1)}, f32[2048,4096]{1,0:T(8,128)}, u32[]{:S(2)}) copy-start(f32[2048,4096]{1,0:T(8,128)} %relation_ref.3) | copy-start | bytes 100663296
  84.9 21.1 %copy-start.11 = (f32[32,32]{1,0:T(8,128)S(1)}, f32[32,32]{1,0:T(8,128)}, u32[]{:S(2)}) copy-start(f32[32,32]{1,0:T(8,128)} %copy-done.10) | copy-start | bytes 12292
  84.9 21.1 %copy-start.13 = (f32[32,32]{1,0:T(8,128)S(1)}, f32[32,32]{1,0:T(8,128)}, u32[]{:S(2)}) copy-start(f32[32,32]{1,0:T(8,128)} %copy-done.12) | copy-start | bytes 12292
  102.3 1.5 collective-permute-start.13
  103.8 7.1 %collective-permute-start.14 = (f32[32,1280]{1,0:T(8,128)S(1)}, f32[32,1280]{1,0:T(8,128)S(1)}, u32[]{:S(2)}, u32[]{:S(2)}) collective-permute-start(f32[32,1280]{1,0:T(8,128)S(1)} %dynamic-slice_add_fusion), channel_id=1, source_target_pairs={{0,2},{1,3},{2,0},{3,1},{4,6},{5,7},{6,4},{7,5},{8,10},{9,11},{10,... | collective-permute-start | bytes 491528 | tf_op jit(solution)/shard_map/ppermute | solution.py:376
  105.9 1.6 copy-start.5
  107.5 0.9 copy-start.7
  109.7 38.9 %copy-start.6 = (bf16[2048,512]{1,0:T(8,128)(2,1)}, bf16[2048,512]{1,0:T(8,128)(2,1)S(1)}, u32[]{:S(2)}) copy-start(bf16[2048,512]{1,0:T(8,128)(2,1)S(1)} %get-tuple-element.40.turned_ref) | copy-start | bytes 6291460
  109.7 38.9 %copy-start.9 = (f32[32,2048]{1,0:T(8,128)}, f32[32,2048]{1,0:T(8,128)S(1)}, u32[]{:S(2)}) copy-start(f32[32,2048]{1,0:T(8,128)S(1)} %get-tuple-element.41.vecs_rows_ref) | copy-start | bytes 786436
  109.7 1.2 collective-permute-start.15
  111.0 1.5 collective-permute-start.20
  112.5 36.1 %copy-start.15 = (f32[32,2048]{1,0:T(8,128)}, f32[32,2048]{1,0:T(8,128)S(1)}, u32[]{:S(2)}) copy-start(f32[32,2048]{1,0:T(8,128)S(1)} %pad_maximum_fusion.3.sums_rows_ref) | copy-start | bytes 786436
  112.5 8.2 %collective-permute-start.23 = (f32[32,2048]{1,0:T(8,128)S(1)}, f32[32,2048]{1,0:T(8,128)S(1)}, u32[]{:S(2)}, u32[]{:S(2)}) collective-permute-start(f32[32,2048]{1,0:T(8,128)S(1)} %pad_maximum_fusion.3.sums_rows_ref), channel_id=1, source_target_pairs={{0,24},{4,28},{9,1},{13,5},{18,10},{22,14},{27,19},{31,23}} | collective-permute-start | bytes 786440 | tf_op jit(solution)/shard_map/ppermute | solution.py:413
  116.8 6.7 %collective-permute-start.22 = (f32[32,2048]{1,0:T(8,128)S(1)}, f32[32,2048]{1,0:T(8,128)S(1)}, u32[]{:S(2)}, u32[]{:S(2)}) collective-permute-start(f32[32,2048]{1,0:T(8,128)S(1)} %pad_maximum_fusion.3.sums_rows_ref), channel_id=1, source_target_pairs={{0,16},{4,20},{9,25},{13,29},{18,2},{22,6},{27,11},{31,15}} | collective-permute-start | bytes 786440 | tf_op jit(solution)/shard_map/ppermute | solution.py:413
  118.1 8.2 %collective-permute-start.21 = (f32[32,2048]{1,0:T(8,128)S(1)}, f32[32,2048]{1,0:T(8,128)S(1)}, u32[]{:S(2)}, u32[]{:S(2)}) collective-permute-start(f32[32,2048]{1,0:T(8,128)S(1)} %pad_maximum_fusion.3.sums_rows_ref), channel_id=1, source_target_pairs={{0,8},{4,12},{9,17},{13,21},{18,26},{22,30},{27,3},{31,7}} | collective-permute-start | bytes 786440 | tf_op jit(solution)/shard_map/ppermute | solution.py:413
  126.3 21.4 %collective-permute-start.24 = (f32[32,2048]{1,0:T(8,128)S(1)}, f32[32,2048]{1,0:T(8,128)S(1)}, u32[]{:S(2)}, u32[]{:S(2)}) collective-permute-start(f32[32,2048]{1,0:T(8,128)S(1)} %add_add_fusion), channel_id=1, source_target_pairs={{0,4},{4,0},{8,12},{12,8},{16,20},{20,16},{24,28},{28,24},{1,5},{5... | collective-permute-start | bytes 786440 | tf_op jit(solution)/shard_map/ppermute | solution.py:426
  127.9 6.4 %collective-permute-start.16 = (f32[32,32]{1,0:T(8,128)S(1)}, f32[32,32]{1,0:T(8,128)S(1)}, u32[]{:S(2)}, u32[]{:S(2)}) collective-permute-start(f32[32,32]{1,0:T(8,128)S(1)} %add.95), channel_id=1, source_target_pairs={{0,2},{1,3},{2,0},{3,1},{4,6},{5,7},{6,4},{7,5},{8,10},{9,11},{10,... | collective-permute-start | bytes 12296 | tf_op jit(solution)/shard_map/ppermute | solution.py:376
  134.4 3.7 %collective-permute-start.17 = (f32[32,32]{1,0:T(8,128)S(1)}, f32[32,32]{1,0:T(8,128)S(1)}, u32[]{:S(2)}, u32[]{:S(2)}) collective-permute-start(f32[32,32]{1,0:T(8,128)S(1)} %add.96), channel_id=1, source_target_pairs={{0,4},{4,0},{8,12},{12,8},{16,20},{20,16},{24,28},{28,24},{1,5},{5... | collective-permute-start | bytes 12296 | tf_op jit(solution)/shard_map/ppermute | solution.py:376
  138.1 3.7 %collective-permute-start.18 = (f32[32,32]{1,0:T(8,128)S(1)}, f32[32,32]{1,0:T(8,128)S(1)}, u32[]{:S(2)}, u32[]{:S(2)}) collective-permute-start(f32[32,32]{1,0:T(8,128)S(1)} %add.97), channel_id=1, source_target_pairs={{0,8},{4,12},{8,0},{12,4},{16,24},{20,28},{24,16},{28,20},{1,9},{5... | collective-permute-start | bytes 12296 | tf_op jit(solution)/shard_map/ppermute | solution.py:376
  141.8 4.6 %collective-permute-start.19 = (f32[32,32]{1,0:T(8,128)S(1)}, f32[32,32]{1,0:T(8,128)S(1)}, u32[]{:S(2)}, u32[]{:S(2)}) collective-permute-start(f32[32,32]{1,0:T(8,128)S(1)} %add.98), channel_id=1, source_target_pairs={{0,16},{4,20},{8,24},{12,28},{16,0},{20,4},{24,8},{28,12},{1,17},{... | collective-permute-start | bytes 12296 | tf_op jit(solution)/shard_map/ppermute | solution.py:376
  148.6 10.5 %copy-start.1 = (f32[2048,4096]{1,0:T(8,128)S(1)}, f32[2048,4096]{1,0:T(8,128)}, u32[]{:S(2)}) copy-start(f32[2048,4096]{1,0:T(8,128)} %relation_ref.3) | copy-start | bytes 100663296

commit v2 on v1

--- a/solution.py
+++ b/solution.py
@@ -47,11 +47,8 @@
     return total
 
 
-ROOM = 30 * 2**20
-
-
-def room(**more):
-    return pltpu.CompilerParams(vmem_limit_bytes=ROOM, **more)
+def room(mebibytes):
+    return pltpu.CompilerParams(vmem_limit_bytes=mebibytes * 2**20)
 
 
 def whole(shape):
@@ -85,9 +82,61 @@
             out_specs=pl.BlockSpec((B, rows), lambda i, place: (0, 0)),
             scratch_shapes=[pltpu.VMEM((width, rows), F32)],
         ),
-        compiler_params=room(),
+        compiler_params=room(40),
         name="strip",
     )(place, source)
+
+
+def hold_kernel(source_ref, held_ref, sem):
+    copy = pltpu.make_async_copy(source_ref, held_ref, sem)
+    copy.start()
+    copy.wait()
+
+
+def hold(source):
+    held = pl.pallas_call(
+        hold_kernel,
+        out_shape=pltpu.VMEM(source.shape, source.dtype),
+        in_specs=[pl.BlockSpec(memory_space=pltpu.HBM)],
+        out_specs=pl.BlockSpec(memory_space=pltpu.VMEM),
+        scratch_shapes=[pltpu.SemaphoreType.DMA],
+        cost_estimate=pl.CostEstimate(
+            flops=0, bytes_accessed=2 * source.size * 4, transcendentals=0
+        ),
+        compiler_params=room(16),
+        name="hold",
+    )(source)
+    return pltpu.with_memory_space_constraint(held, pltpu.VMEM)
+
+
+def grow_kernel(turned_ref, scaled_ref, relation_ref, grown_ref):
+    step = relation_ref.shape[0]
+    here = pl.ds(pl.multiple_of(pl.program_id(0) * step, step), step)
+    grown_ref[here, :] = relation_ref[...] + jnp.dot(
+        turned_ref[...], scaled_ref[...], preferred_element_type=F32
+    )
+
+
+def grow(turned, scaled, relation):
+    rows, width = relation.shape
+    step = min(256, rows)
+    grown = pl.pallas_call(
+        grow_kernel,
+        out_shape=pltpu.VMEM((rows, width), F32),
+        grid=(rows // step,),
+        in_specs=[
+            pl.BlockSpec((step, M), lambda i: (i, 0)),
+            pl.BlockSpec((M, width), lambda i: (0, 0), pipeline_mode=pl.Buffered(1)),
+            pl.BlockSpec((step, width), lambda i: (i, 0)),
+        ],
+        out_specs=pl.BlockSpec(memory_space=pltpu.VMEM),
+        cost_estimate=pl.CostEstimate(
+            flops=2 * M * rows * width, bytes_accessed=8 * rows * width, transcendentals=0
+        ),
+        compiler_params=room(20),
+        name="grow",
+    )(turned, scaled, relation)
+    return pltpu.with_memory_space_constraint(grown, pltpu.VMEM)
 
 
 def lifted(strip, ids, factor, lift):
@@ -138,7 +187,7 @@
             in_specs=[whole(raw.shape), whole(chosen.shape), whole(scaled.shape)],
             out_specs=(whole((B, width)), whole((2 * B, B))),
         ),
-        compiler_params=room(),
+        compiler_params=room(8),
         name="panel",
     )(place, raw, chosen, scaled)
 
@@ -201,19 +250,24 @@
         cost_estimate=pl.CostEstimate(
             flops=16 * B * rows * width, bytes_accessed=4 * rows * width, transcendentals=0
         ),
-        compiler_params=room(),
+        compiler_params=room(16),
         name="product",
     )(place, strip, factor, lift, scaled, relation)
 
 
 def rows_kernel(
-    place_ref, raw_ref, chosen_ref, scaled_ref, factor_ref, lift_ref, sums_ref,
+    place_ref, raw_ref, chosen_ref, mine_ref, other_ref, factor_ref, lift_ref, sums_ref,
     vecs_ref, inner_ref, turned_ref,
 ):
-    scaled = scaled_ref[...]
-    strip = raw_ref[...] + jnp.dot(
-        chosen_ref[...], scaled, preferred_element_type=F32
-    ) * (1.0 / M)
+    even = place_ref[1] == 0
+    mine, other = mine_ref[...], other_ref[...]
+    first = jnp.where(even, mine, other)
+    second = jnp.where(even, other, mine)
+    half = M // 2
+    grown = jnp.dot(
+        chosen_ref[:, :half], first, preferred_element_type=F32
+    ) + jnp.dot(chosen_ref[:, half:], second, preferred_element_type=F32)
+    strip = raw_ref[...] + grown * (1.0 / M)
     ids = lane_ids(strip.shape[1], place_ref[0])
     vecs = lifted(strip, ids, factor_ref[...], lift_ref[...])
     vecs_ref[...] = vecs
@@ -224,12 +278,13 @@
         preferred_element_type=F32,
     )
     inner_ref[...] = fold(square[:, :B] + square[:, B:], 2)
-    turned_ref[...] = (scaled.astype(F32) * (1.0 / M)).T.astype(BF16)
-
-
-def row_block(place, raw, chosen, scaled, factor, lift, sums):
-    args = (raw, chosen, scaled, factor, lift, sums)
-    outs = ((raw.shape, F32), ((B, B), F32), (scaled.shape[::-1], BF16))
+    turned_ref[:, :half] = (first.astype(F32) * (1.0 / M)).T.astype(BF16)
+    turned_ref[:, half:] = (second.astype(F32) * (1.0 / M)).T.astype(BF16)
+
+
+def row_block(place, raw, chosen, mine, other, factor, lift, sums):
+    args = (raw, chosen, mine, other, factor, lift, sums)
+    outs = ((raw.shape, F32), ((B, B), F32), ((raw.shape[1], M), BF16))
     return pl.pallas_call(
         rows_kernel,
         out_shape=tuple(jax.ShapeDtypeStruct(*out) for out in outs),
@@ -239,7 +294,7 @@
             in_specs=[whole(a.shape) for a in args],
             out_specs=tuple(whole(out[0]) for out in outs),
         ),
-        compiler_params=room(),
+        compiler_params=room(14),
         name="rows",
     )(place, *args)
 
@@ -286,22 +341,22 @@
 def reflect(small):
     out = jax.ShapeDtypeStruct((B, B), F32)
     return pl.pallas_call(
-        reflect_kernel, out_shape=(out,) * 3, compiler_params=room(), name="reflect"
+        reflect_kernel, out_shape=(out,) * 3, compiler_params=room(2), name="reflect"
     )(small)
 
 
 def update_kernel(
-    triangle_ref, inner_ref, marks_ref, turned_ref, scaled_rows_ref, vecs_rows_ref,
-    sums_rows_ref, scaled_cols_ref, vecs_cols_ref, sums_cols_ref, relation_ref,
+    triangle_ref, inner_ref, marks_ref, turned_ref, vecs_rows_ref, sums_rows_ref,
+    scaled_cols_ref, vecs_cols_ref, sums_cols_ref, relation_ref,
     out_ref, left_ref, half_ref,
 ):
     def dot(a, b, dims):
         return lax.dot_general(a, b, dims, precision=HIGH, preferred_element_type=F32)
 
-    def parts(vecs, sums, scaled):
-        marks = jnp.concatenate(split(marks_ref[...] * (1.0 / M)), axis=0)
+    def parts(vecs, sums, scaled, dims, scale):
+        marks = jnp.concatenate(split(marks_ref[...] * scale), axis=0)
         full = sums + fold(
-            lax.dot_general(marks, scaled, NN, preferred_element_type=F32), 2
+            lax.dot_general(marks, scaled, dims, preferred_element_type=F32), 2
         )
         th, tl = split(triangle_ref[...])
         hh, hl = split(-half_ref[...])
@@ -322,13 +377,15 @@
         inner = inner_ref[...] + dot(marks, marks, NT) * (1.0 / M)
         half_ref[...] = 0.5 * dot(triangle, dot(inner, triangle, NN), TN)
         vh, vl, ah, al = parts(
-            vecs_rows_ref[...], sums_rows_ref[...], scaled_rows_ref[...]
+            vecs_rows_ref[...], sums_rows_ref[...], turned_ref[...], NT, 1.0
         )
         left = jnp.concatenate([vh, vh, vl, vl, ah, ah, al, al], axis=0)
         left_ref[...] = left.astype(F32).T.astype(BF16)
 
     scaled = scaled_cols_ref[...]
-    vh, vl, ah, al = parts(vecs_cols_ref[...], sums_cols_ref[...], scaled)
+    vh, vl, ah, al = parts(
+        vecs_cols_ref[...], sums_cols_ref[...], scaled, NN, 1.0 / M
+    )
     right = -jnp.concatenate([ah, al, ah, al, vh, vl, vh, vl], axis=0)
     rows, step = out_ref.shape
     here = pl.ds(pl.multiple_of(pl.program_id(0) * step, step), step)
@@ -337,7 +394,6 @@
         some = pl.ds(k * chunk, chunk)
         out_ref[some, :] = (
             relation_ref[some, here]
-            + jnp.dot(turned_ref[some, :], scaled, preferred_element_type=F32)
             + jnp.dot(left_ref[some, :], right, preferred_element_type=F32)
         )
 
@@ -363,11 +419,11 @@
         out_specs=slab(relation),
         scratch_shapes=[pltpu.VMEM((rows, 8 * B), BF16), pltpu.VMEM((B, B), F32)],
         cost_estimate=pl.CostEstimate(
-            flops=2 * (M + 8 * B) * rows * width,
-            bytes_accessed=8 * rows * width,
+            flops=16 * B * rows * width,
+            bytes_accessed=4 * rows * width,
             transcendentals=0,
         ),
-        compiler_params=room(),
+        compiler_params=room(20),
         name="update",
     )(*fixed, *of_cols, relation)
 
@@ -393,15 +449,42 @@
         panel_col = place * B // tile_cols
         panel_off = place * B % tile_cols
         own_col = row_id // per
-
-        def from_panel(value, bits):
-            for bit in bits:
-                other = swap(value, "col", n_col, bit)
-                value = jnp.where(((col_id ^ panel_col) & bit) != 0, other, value)
+        mine = row_id % per
+
+        raw_rows = take_strip(relation, panel_off)
+        apart = col_id ^ own_col
+        place_cols = jnp.reshape(col_id * tile_cols - first_row, (1,)).astype(jnp.int32)
+        place_rows = jnp.stack([row_id * tile_rows - first_row, col_id % 2]).astype(jnp.int32)
+        even = col_id % 2 == 0
+        at_own = own_col == col_id
+        is_mine = [mine == s for s in range(per)]
+        from_bit = [((col_id ^ panel_col) & bit) != 0 for bit in bits_of(n_col)]
+        take_bit = [(apart & bit) != 0 for bit in bits_of(n_col)]
+        shifts = [[(mine ^ s) == shift for shift in range(per)] for s in range(per)]
+        scalars = (place_cols, place_rows, even, at_own, is_mine, from_bit, take_bit, shifts)
+        ready, scalars = lax.optimization_barrier((relation, scalars))
+        place_cols, place_rows, even, at_own, is_mine, from_bit, take_bit, shifts = scalars
+
+        def from_panel(value, first, last):
+            for k in range(first, last):
+                other = swap(value, "col", n_col, 1 << k)
+                value = jnp.where(from_bit[k], other, value)
             return value
 
+        def halves(value, axis):
+            size = value.shape[axis] // 2
+            one = lax.slice_in_dim(value, 0, size, axis=axis)
+            two = lax.slice_in_dim(value, size, 2 * size, axis=axis)
+            return jnp.where(even, one, two), jnp.where(even, two, one)
+
+        def rejoin(value, axis):
+            other = swap(value, "col", n_col, 1)
+            return jnp.concatenate(
+                [jnp.where(even, value, other), jnp.where(even, other, value)], axis=axis
+            )
+
         def to_column(block):
-            total = jnp.where(own_col == col_id, block, 0.0)
+            total = jnp.where(at_own, block, 0.0)
             received = []
             for shift in range(1, n_col):
                 pairs = []
@@ -416,7 +499,6 @@
             return total
 
         def join_column(block):
-            mine = row_id % per
             parts = [None] * per
             got = [block]
             for shift in range(1, per):
@@ -427,20 +509,21 @@
             for s in range(per):
                 value = got[0]
                 for shift in range(1, per):
-                    value = jnp.where((mine ^ s) == shift, got[shift], value)
+                    value = jnp.where(shifts[s][shift], got[shift], value)
                 parts[s] = value
             return jnp.concatenate(parts, axis=1)
 
-        raw_rows = take_strip(relation, panel_off)
-        held = pltpu.with_memory_space_constraint(relation, pltpu.VMEM)
-        raw_rows = from_panel(raw_rows, [1])
+        log_col = n_col.bit_length() - 1
+        raw_rows = from_panel(raw_rows, 0, 1)
         dosage, raw_rows = lax.optimization_barrier((dosage, raw_rows))
         scaled = standardize(dosage, freq)
         chosen = take_strip(dosage, panel_off)
-        chosen = from_panel(standardize(chosen, freq, 0), bits_of(n_col))
-        raw_rows = from_panel(raw_rows, bits_of(n_col)[1:])
-
-        own = lax.dynamic_slice_in_dim(scaled, (row_id % per) * tile_rows, tile_rows, 1)
+        chosen = from_panel(standardize(chosen, freq, 0), 0, log_col)
+        raw_rows = from_panel(raw_rows, 1, log_col)
+
+        own = scaled[:, :tile_rows]
+        for k in range(1, per):
+            own = jnp.where(is_mine[k], scaled[:, k * tile_rows : (k + 1) * tile_rows], own)
 
         def spread_rows(value, bit):
             pairs = []
@@ -453,64 +536,58 @@
                     elif (apart & ~1) & ~(bit - 1) == 0:
                         pairs.append((r * n_col + c, r * n_col + (c ^ bit)))
             other = lax.ppermute(value, both, pairs)
-            apart = col_id ^ own_col
-            if bit == 1:
-                take = (apart & 1) != 0
-            else:
-                take = (apart & bit) != 0
-            return jnp.where(take, other, value)
+            return jnp.where(take_bit[bit.bit_length() - 1], other, value)
 
         own = spread_rows(own, 1)
-        core = col_id % 2
-        half = M // 2
-        part = lax.dynamic_slice_in_dim(own, core * half, half, 0)
-        part, raw_rows = lax.optimization_barrier((part, raw_rows))
+        part, _ = halves(own, 0)
+        part, raw_rows, ready = lax.optimization_barrier((part, raw_rows, ready))
         for bit in bits_of(n_col)[1:]:
             part = spread_rows(part, bit)
-        other = swap(part, "col", n_col, 1)
-        rows_scaled = jnp.concatenate(
-            [jnp.where(core == 0, part, other), jnp.where(core == 0, other, part)], axis=0
-        )
-
-        raw_cols = join_column(to_column(raw_rows))
-        place_cols = jnp.reshape(col_id * tile_cols - first_row, (1,)).astype(jnp.int32)
-        place_rows = jnp.reshape(row_id * tile_rows - first_row, (1,)).astype(jnp.int32)
+        other_part = swap(part, "col", n_col, 1)
+
+        raw_cols, held = lax.optimization_barrier((to_column(raw_rows), hold(ready)))
+        raw_cols = join_column(raw_cols)
         strip_cols, small = panel_block(place_cols, raw_cols, chosen, scaled)
         for bit in bits_of(n_col):
             small = small + swap(small, "col", n_col, bit)
-        small, rows_scaled = lax.optimization_barrier((small, rows_scaled))
+        small, other_part = lax.optimization_barrier((small, other_part))
         factor, lift, triangle = reflect(small)
 
         vecs_cols, part_sums, part_marks = tile_product(
             place_cols, strip_cols, factor, lift, scaled, held
         )
-        sums = jnp.concatenate([part_sums, part_marks], axis=1)
-        width = sums.shape[1] // 2
-        kept = lax.dynamic_slice_in_dim(sums, core * width, width, 1)
-        sent = lax.dynamic_slice_in_dim(sums, (1 - core) * width, width, 1)
         vecs_rows, inner, turned = row_block(
-            place_rows, raw_rows, chosen, rows_scaled, factor, lift, part_sums
-        )
+            place_rows, raw_rows, chosen, part, other_part, factor, lift, part_sums
+        )
+        kept, sent = halves(jnp.concatenate([part_sums, part_marks], axis=1), 1)
+        kept = jnp.concatenate([kept, inner], axis=1)
+        sent = jnp.concatenate([sent, inner], axis=1)
         kept = kept + swap(sent, "col", n_col, 1)
-        inner = inner + swap(inner, "col", n_col, 1)
         for bit in bits_of(n_col)[1:]:
-            other = swap(kept, "col", n_col, bit)
-            other, inner = lax.optimization_barrier((other, inner))
-            kept = kept + other
-            inner = inner + swap(inner, "col", n_col, bit)
-        other = swap(kept, "col", n_col, 1)
-        sums = jnp.concatenate(
-            [jnp.where(core == 0, kept, other), jnp.where(core == 0, other, kept)], axis=1
-        )
+            kept = kept + swap(kept, "col", n_col, bit)
+        inner = kept[:, -B:]
+        sums = rejoin(kept[:, :-B], 1)
         sums_rows, marks = sums[:, :tile_rows], sums[:, tile_rows:]
-        for bit in bits_of(n_row):
-            inner = inner + swap(inner, "row", n_row, bit)
-        sums_cols = join_column(to_column(sums_rows))
+
+        near = inner
+        for shift in range(1, per):
+            pairs = [(r, (r // per) * per + (r % per) ^ shift) for r in range(n_row)]
+            near = near + lax.ppermute(inner, "row", pairs)
+        sums_rows, ready, turned = lax.optimization_barrier((sums_rows, ready, turned))
+        ready, near = lax.optimization_barrier((ready, near))
+        sums_cols, held, near = lax.optimization_barrier(
+            (to_column(sums_rows), grow(turned, scaled, ready), near)
+        )
+        inner = near
+        for shift in range(1, n_col):
+            pairs = [(r, (r + shift * per) % n_row) for r in range(n_row)]
+            inner = inner + lax.ppermute(near, "row", pairs)
+        sums_cols = join_column(sums_cols)
         return tile_update(
             triangle,
             inner,
             marks,
-            (turned, rows_scaled, vecs_rows, sums_rows),
+            (turned, vecs_rows, sums_rows),
             (scaled, vecs_cols, sums_cols),
             held,
         )

time: 182 us -> 142 us (0.78)
  local copies, waits for them, and re-layouts: 35.5 us -> 0.05 us
  Pallas kernels: 50.5 us -> 70.9 us
  waiting for transfers between devices: 45.8 us -> 31.6 us
  starting transfers between devices: 38.6 us -> 31.7 us
  other arithmetic: 10.2 us -> 6.09 us
    unnamed x35 -> x10, local copies, waits for them, and re-layouts: 32.5 us -> 0.03 us
    pallas_call x0 -> x2, Pallas kernels: none -> 27.9 us  [the longest x1 17.4 us: grow(): pl.pallas_call(grow_kernel, out_shape=pltpu.VMEM((rows, width), F32), gri...]
    ppermute x6, waiting for transfers between devices: 12.2 us -> 0.02 us  [to_column(): received.append(lax.ppermute(block, both, pairs))]
    ppermute x15 -> x10, waiting for transfers between devices: 29.1 us -> 18.7 us  [swap(): return lax.ppermute(value, axis, [(i, i ^ bit) for i in range(size)])]
    ppermute x15 -> x10, starting transfers between devices: 14.8 us -> 5.54 us  [swap(): return lax.ppermute(value, axis, [(i, i ^ bit) for i in range(size)])]
    ppermute x0 -> x4, waiting for transfers between devices: none -> 6.37 us  [the longest x3 4.24 us: body(): inner = inner + lax.ppermute(near, 'row', pairs)]
    pallas_call x1, Pallas kernels: 22.4 us -> 17 us  [tile_update(): pl.pallas_call(update_kernel, out_shape=jax.ShapeDtypeStruct((rows, width...]
    ppermute x2, waiting for transfers between devices: 1.26 us -> 5.01 us  [join_column(): got.append(lax.ppermute(block, 'row', pairs))]
  transfers between devices with their start and end apart: 25 -> 24, of which waited for: 20 -> 14; matrix products, arithmetic and copies ran while one was open for 1% -> 0% of each run, Pallas kernels for 2% -> 21%
where the time goes in v2:
time: 142 us; the launch traced here: 141 us
  Pallas kernels  70.9 us (50%)
  starting transfers between devices  31.7 us (22%)
  waiting for transfers between devices  31.6 us (22%)
  other arithmetic  6.09 us (4%)
    ppermute x10, waiting for transfers between devices, swap(): return lax.ppermute(value, axis, [(i, i ^ bit) for i in range(size)])  18.7 us
    pallas_call x1, Pallas kernels, grow(): pl.pallas_call(grow_kernel, out_shape=pltpu.VMEM((rows, width), F32), gri...  17.4 us
    pallas_call x1, Pallas kernels, tile_update(): pl.pallas_call(update_kernel, out_shape=jax.ShapeDtypeStruct((rows, width...  17 us
    pallas_call x1, Pallas kernels, tile_product(): pl.pallas_call(product_kernel, out_shape=(jax.ShapeDtypeStruct((B, width)...  12.9 us
    ppermute x6, starting transfers between devices, to_column(): received.append(lax.ppermute(block, both, pairs))  12.8 us
    pallas_call x1, Pallas kernels, hold(): pl.pallas_call(hold_kernel, out_shape=pltpu.VMEM(source.shape, source.dty...  10.6 us
    pallas_call x1, Pallas kernels, reflect(): pl.pallas_call(reflect_kernel, out_shape=(out,) * 3, compiler_params=room...  7.13 us
    ppermute x2, starting transfers between devices, spread_rows(): other = lax.ppermute(value, both, pairs)  6.65 us
  transfers between devices with their start and end apart: 24, of which 14 were waited for; matrix products, arithmetic and copies ran while one was open for 0% of the time, Pallas kernels for 21%

profile of v2, /device:TPU:0, one launch (start us, length us, event | category | flops | bytes accessed | tf_op | source)
XLA Modules:
  0.0 141.5 jit_solution(11056569741931137671)
XLA Ops:
  0.7 0.1 pad_add_fusion.1.place_ref
  0.8 2.1 %strip.2 = f32[32,2048]{1,0:T(8,128)S(1)} custom-call(s32[2]{0:T(128)S(1)} %pad_add_fusion.1.place_ref, f32[2048,4096]{1,0:T(8,128)} %relation_ref), custom_call_target="tpu_custom_call" | custom-call | tf_op jit(solution)/shard_map/strip/pallas_call | solution.py:75
  2.9 0.6 collective-permute-start
  3.5 0.1 pad_add_fusion.place_ref
  3.5 1.1 collective-permute-done
  4.7 4.4 %divide_convert_fusion.scaled_ref.scaled_cols_ref = bf16[512,4096]{1,0:T(8,128)(2,1)S(1)} fusion(s32[512,4096]{1,0:T(8,128)} %source_ref.3, f32[512]{0:T(512)S(1)} %get-tuple-element.94, f32[512]{0:T(512)S(1)} %get-tuple-element.93), kind=kLoop, calls=%fused_computation | loop fusion | flops 10485760 | bytes 12587008 | tf_op jit(solution)/shard_map/convert_element_type | solution.py:63
  9.0 0.0 slice-start
  9.1 0.2 slice_select_fusion
  9.3 2.8 %collective-permute-start.1 = (bf16[512,2048]{1,0:T(8,128)(2,1)S(1)}, bf16[512,2048]{1,0:T(8,128)(2,1)S(1)}, u32[]{:S(2)}, u32[]{:S(2)}) collective-permute-start(bf16[512,2048]{1,0:T(8,128)(2,1)S(1)} %slice_select_fusion), channel_id=1, source_target_pairs={{0,1},{4,5},{9,8},{13,12},{18,19},{22,23},{27,26},{31,30}} | collective-permute-start | bytes 6291464 | tf_op jit(solution)/shard_map/ppermute | solution.py:538
  12.1 1.0 collective-permute-start.2
  13.1 6.6 %collective-permute-done.2 = f32[32,2048]{1,0:T(8,128)S(1)} collective-permute-done((f32[32,2048]{1,0:T(8,128)S(1)}, f32[32,2048]{1,0:T(8,128)S(1)}, u32[]{:S(2)}, u32[]{:S(2)}) %collective-permute-start.2) | collective-permute-done | bytes 262176 | tf_op jit(solution)/shard_map/ppermute | solution.py:432
  19.8 0.0 slice-start.1
  19.8 0.0 collective-permute-done.1
  19.8 0.5 broadcast_select_fusion
  20.3 0.1 slice_select_fusion.1
  20.5 3.8 %collective-permute-start.11 = (bf16[256,2048]{1,0:T(8,128)(2,1)S(1)}, bf16[256,2048]{1,0:T(8,128)(2,1)S(1)}, u32[]{:S(2)}, u32[]{:S(2)}) collective-permute-start(bf16[256,2048]{1,0:T(8,128)(2,1)S(1)} %slice_select_fusion.1), channel_id=1, source_target_pairs={{0,2},{1,3},{4,6},{5,7},{8,10},{9,11},{12,14},{13,15},{18,16},{19,... | collective-permute-start | bytes 3145736 | tf_op jit(solution)/shard_map/ppermute | solution.py:538
  24.3 0.7 strip.3
  25.0 3.6 %collective-permute-start.5 = (f32[32,2048]{1,0:T(8,128)S(1)}, f32[32,2048]{1,0:T(8,128)S(1)}, u32[]{:S(2)}, u32[]{:S(2)}) collective-permute-start(f32[32,2048]{1,0:T(8,128)S(1)} %broadcast_select_fusion.4.raw_ref), channel_id=1, source_target_pairs={{0,24},{4,28},{9,1},{13,5},{18,10},{22,14},{27,19},{31,23}} | collective-permute-start | bytes 786440 | tf_op jit(solution)/shard_map/ppermute | solution.py:496
  28.7 1.3 collective-permute-start.4
  30.0 1.3 collective-permute-start.3
  31.3 0.1 collective-permute-start.7
  31.4 1.2 collective-permute-done.7
  32.6 0.1 collective-permute-start.8
  32.7 10.6 %hold.1.relation_ref = f32[2048,4096]{1,0:T(8,128)S(1)} custom-call(f32[2048,4096]{1,0:T(8,128)} %relation_ref), custom_call_target="tpu_custom_call" | custom-call | bytes 67108864 | tf_op jit(solution)/shard_map/hold/pallas_call | solution.py:97
  43.3 0.0 collective-permute-done.5
  43.3 0.0 collective-permute-done.4
  43.3 0.0 collective-permute-done.3
  43.3 0.1 add_add_fusion.1
  43.4 1.6 %collective-permute-start.6 = (f32[32,2048]{1,0:T(8,128)S(1)}, f32[32,2048]{1,0:T(8,128)S(1)}, u32[]{:S(2)}, u32[]{:S(2)}) collective-permute-start(f32[32,2048]{1,0:T(8,128)S(1)} %add_add_fusion.1), channel_id=1, source_target_pairs={{0,4},{4,0},{8,12},{12,8},{16,20},{20,16},{24,28},{28,24},{1,5},{5... | collective-permute-start | bytes 786440 | tf_op jit(solution)/shard_map/ppermute | solution.py:508
  45.0 1.5 %collective-permute-done.11 = bf16[256,2048]{1,0:T(8,128)(2,1)S(1)} collective-permute-done((bf16[256,2048]{1,0:T(8,128)(2,1)S(1)}, bf16[256,2048]{1,0:T(8,128)(2,1)S(1)}, u32[]{:S(2)}, u32[]{:S(2)}) %collective-permute-start.11) | collective-permute-done | bytes 1048608 | tf_op jit(solution)/shard_map/ppermute | solution.py:538
  46.4 0.1 broadcast_select_fusion.1.mine_ref
  46.6 0.1 collective-permute-start.12
  46.7 0.1 collective-permute-done.8
  46.8 5.0 %collective-permute-done.6 = f32[32,2048]{1,0:T(8,128)S(1)} collective-permute-done((f32[32,2048]{1,0:T(8,128)S(1)}, f32[32,2048]{1,0:T(8,128)S(1)}, u32[]{:S(2)}, u32[]{:S(2)}) %collective-permute-start.6) | collective-permute-done | bytes 262176 | tf_op jit(solution)/shard_map/ppermute | solution.py:508
  51.9 1.3 panel.1
  53.2 0.1 collective-permute-start.9
  53.3 1.2 collective-permute-done.9
  54.5 1.7 %collective-permute-start.10 = (f32[64,32]{1,0:T(8,128)S(1)}, f32[64,32]{1,0:T(8,128)S(1)}, u32[]{:S(2)}, u32[]{:S(2)}) collective-permute-start(f32[64,32]{1,0:T(8,128)S(1)} %add.72), channel_id=1, source_target_pairs={{0,2},{1,3},{2,0},{3,1},{4,6},{5,7},{6,4},{7,5},{8,10},{9,11},{10,... | collective-permute-start | bytes 24584 | tf_op jit(solution)/shard_map/ppermute | solution.py:432
  56.2 2.2 %collective-permute-done.10 = f32[64,32]{1,0:T(8,128)S(1)} collective-permute-done((f32[64,32]{1,0:T(8,128)S(1)}, f32[64,32]{1,0:T(8,128)S(1)}, u32[]{:S(2)}, u32[]{:S(2)}) %collective-permute-start.10) | collective-permute-done | bytes 8224 | tf_op jit(solution)/shard_map/ppermute | solution.py:432
  58.4 7.1 %reflect.1 = (f32[32,32]{1,0:T(8,128)S(1)}, f32[32,32]{1,0:T(8,128)S(1)}, f32[32,32]{1,0:T(8,128)S(1)}) custom-call(f32[64,32]{1,0:T(8,128)S(1)} %add.73.small_ref), custom_call_target="tpu_custom_call" | custom-call | tf_op jit(solution)/shard_map/reflect/pallas_call | solution.py:343
  65.6 12.9 %product.1 = (f32[32,4096]{1,0:T(8,128)S(1)}, f32[32,2048]{1,0:T(8,128)S(1)}, f32[32,512]{1,0:T(8,128)S(1)}) custom-call(s32[1]{0:T(128)} %bitcast.1.place_ref, f32[32,4096]{1,0:T(8,128)S(1)} %get-tuple-element.65.strip_ref, f32[32,32]{1,0:T(8,128)S(1)} %get-tuple-element.66.factor_ref, f32[32,32]{1,0:T(8,128)S(1)} %get-tuple-element.67.lift_ref, ...), custom_call_target="tpu_custom_call" | custom-call | flops 4294967296 | bytes 33554432 | tf_op jit(solution)/shard_map/product/pallas_call | solution.py:226
  78.4 1.9 %rows.1 = (f32[32,2048]{1,0:T(8,128)S(1)}, f32[32,32]{1,0:T(8,128)S(1)}, bf16[2048,512]{1,0:T(8,128)(2,1)S(1)}) custom-call(s32[2]{0:T(128)S(1)} %pad_add_fusion.place_ref, f32[32,2048]{1,0:T(8,128)S(1)} %broadcast_select_fusion.4.raw_ref, bf16[32,512]{1,0:T(8,128)(2,1)S(1)} %broadcast_select_fusion.11.chosen_ref, ...), custom_call_target="tpu_custom_call" | custom-call | tf_op jit(solution)/shard_map/rows/pallas_call | solution.py:288
  80.4 0.1 collective-permute-start.13
  80.5 1.4 collective-permute-done.13
  81.9 1.8 %collective-permute-start.14 = (f32[32,1312]{1,0:T(8,128)S(1)}, f32[32,1312]{1,0:T(8,128)S(1)}, u32[]{:S(2)}, u32[]{:S(2)}) collective-permute-start(f32[32,1312]{1,0:T(8,128)S(1)} %fusion), channel_id=1, source_target_pairs={{0,2},{1,3},{2,0},{3,1},{4,6},{5,7},{6,4},{7,5},{8,10},{9,11},{10,... | collective-permute-start | bytes 503816 | tf_op jit(solution)/shard_map/ppermute | solution.py:432
  83.7 4.9 %collective-permute-done.14 = f32[32,1312]{1,0:T(8,128)S(1)} collective-permute-done((f32[32,1312]{1,0:T(8,128)S(1)}, f32[32,1312]{1,0:T(8,128)S(1)}, u32[]{:S(2)}, u32[]{:S(2)}) %collective-permute-start.14) | collective-permute-done | bytes 167968 | tf_op jit(solution)/shard_map/ppermute | solution.py:432
  88.6 1.6 %collective-permute-start.19 = (f32[32,32]{1,0:T(8,128)S(1)}, f32[32,32]{1,0:T(8,128)S(1)}, u32[]{:S(2)}, u32[]{:S(2)}) collective-permute-start(f32[32,32]{1,0:T(8,128)S(1)} %slice.45), channel_id=1, source_target_pairs={{0,4},{4,0},{8,12},{12,8},{16,20},{20,16},{24,28},{28,24},{1,5},{5... | collective-permute-start | bytes 12296 | tf_op jit(solution)/shard_map/ppermute | solution.py:575
  90.2 0.1 collective-permute-start.15
  90.3 2.1 %collective-permute-done.19 = f32[32,32]{1,0:T(8,128)S(1)} collective-permute-done((f32[32,32]{1,0:T(8,128)S(1)}, f32[32,32]{1,0:T(8,128)S(1)}, u32[]{:S(2)}, u32[]{:S(2)}) %collective-permute-start.19) | collective-permute-done | bytes 4128 | tf_op jit(solution)/shard_map/ppermute | solution.py:575
  92.4 0.0 collective-permute-done.15
  92.5 3.7 %collective-permute-start.18 = (f32[32,2048]{1,0:T(8,128)S(1)}, f32[32,2048]{1,0:T(8,128)S(1)}, u32[]{:S(2)}, u32[]{:S(2)}) collective-permute-start(f32[32,2048]{1,0:T(8,128)S(1)} %pad_maximum_fusion.2.sums_rows_ref), channel_id=1, source_target_pairs={{0,24},{4,28},{9,1},{13,5},{18,10},{22,14},{27,19},{31,23}} | collective-permute-start | bytes 786440 | tf_op jit(solution)/shard_map/ppermute | solution.py:496
  96.2 1.3 collective-permute-start.17
  97.6 1.5 %collective-permute-start.16 = (f32[32,2048]{1,0:T(8,128)S(1)}, f32[32,2048]{1,0:T(8,128)S(1)}, u32[]{:S(2)}, u32[]{:S(2)}) collective-permute-start(f32[32,2048]{1,0:T(8,128)S(1)} %pad_maximum_fusion.2.sums_rows_ref), channel_id=1, source_target_pairs={{0,8},{4,12},{9,17},{13,21},{18,26},{22,30},{27,3},{31,7}} | collective-permute-start | bytes 786440 | tf_op jit(solution)/shard_map/ppermute | solution.py:496
  99.1 17.4 %grow.1.relation_ref = f32[2048,4096]{1,0:T(8,128)S(1)} custom-call(bf16[2048,512]{1,0:T(8,128)(2,1)} %copy-done.1, bf16[512,4096]{1,0:T(8,128)(2,1)} %copy-done, f32[2048,4096]{1,0:T(8,128)} %relation_ref), custom_call_target="tpu_custom_call" | custom-call | flops 8589934592 | bytes 67108864 | tf_op jit(solution)/shard_map/grow/pallas_call | solution.py:123
  116.5 0.0 collective-permute-done.17
  116.5 0.0 collective-permute-done.16
  116.5 0.1 add_add_fusion
  116.6 1.6 %collective-permute-start.23 = (f32[32,2048]{1,0:T(8,128)S(1)}, f32[32,2048]{1,0:T(8,128)S(1)}, u32[]{:S(2)}, u32[]{:S(2)}) collective-permute-start(f32[32,2048]{1,0:T(8,128)S(1)} %add_add_fusion), channel_id=1, source_target_pairs={{0,4},{4,0},{8,12},{12,8},{16,20},{20,16},{24,28},{28,24},{1,5},{5... | collective-permute-start | bytes 786440 | tf_op jit(solution)/shard_map/ppermute | solution.py:508
  118.1 2.0 %collective-permute-start.20 = (f32[32,32]{1,0:T(8,128)S(1)}, f32[32,32]{1,0:T(8,128)S(1)}, u32[]{:S(2)}, u32[]{:S(2)}) collective-permute-start(f32[32,32]{1,0:T(8,128)S(1)} %slice_add_fusion), channel_id=1, source_target_pairs={{0,8},{4,12},{8,16},{12,20},{16,24},{20,28},{24,0},{28,4},{1,9},{5... | collective-permute-start | bytes 12296 | tf_op jit(solution)/shard_map/ppermute | solution.py:584
  120.2 1.7 %collective-permute-done.22 = f32[32,32]{1,0:T(8,128)S(1)} collective-permute-done((f32[32,32]{1,0:T(8,128)S(1)}, f32[32,32]{1,0:T(8,128)S(1)}, u32[]{:S(2)}, u32[]{:S(2)}) %collective-permute-start.22) | collective-permute-done | bytes 4128 | tf_op jit(solution)/shard_map/ppermute | solution.py:584
  121.9 0.9 collective-permute-done.21
  122.8 1.6 %collective-permute-done.20 = f32[32,32]{1,0:T(8,128)S(1)} collective-permute-done((f32[32,32]{1,0:T(8,128)S(1)}, f32[32,32]{1,0:T(8,128)S(1)}, u32[]{:S(2)}, u32[]{:S(2)}) %collective-permute-start.20) | collective-permute-done | bytes 4128 | tf_op jit(solution)/shard_map/ppermute | solution.py:584
  124.4 0.0 collective-permute-done.23
  124.5 17.0 %update.1 = f32[2048,4096]{1,0:T(8,128)} custom-call(f32[32,32]{1,0:T(8,128)S(1)} %get-tuple-element.64.triangle_ref, f32[32,32]{1,0:T(8,128)S(1)} %add_add_fusion.2.inner_ref, f32[32,512]{1,0:T(8,128)S(1)} %slice.46.marks_ref, bf16[2048,512]{1,0:T(8,128)(2,1)} %copy-done.1, f32[32,2048]{1,0:T(8,128)S(1)} %get-tuple-element.81.vecs_rows_ref, ...), custom_call_target="tpu_custom_call" | custom-call | flops 4294967296 | bytes 33554432 | tf_op jit(solution)/shard_map/update/pallas_call | solution.py:412
  (36 shorter events, 0.5 us)
Async XLA Ops:
  0.8 2.8 %copy-start.2 = (s32[512]{0:T(512)S(1)}, s32[512]{0:T(512)}, u32[]{:S(2)}) copy-start(s32[512]{0:T(512)} %param.6) | copy-start | bytes 6148
  2.9 1.7 %collective-permute-start = (f32[32,2048]{1,0:T(8,128)S(1)}, f32[32,2048]{1,0:T(8,128)S(1)}, u32[]{:S(2)}, u32[]{:S(2)}) collective-permute-start(f32[32,2048]{1,0:T(8,128)S(1)} %strip.2), channel_id=1, source_target_pairs={{0,1},{1,0},{2,3},{3,2},{4,5},{5,4},{6,7},{7,6},{8,9},{9,8},{10,11... | collective-permute-start | bytes 786440 | tf_op jit(solution)/shard_map/ppermute | solution.py:432
  9.0 56.5 %copy-start = (bf16[512,4096]{1,0:T(8,128)(2,1)}, bf16[512,4096]{1,0:T(8,128)(2,1)S(1)}, u32[]{:S(2)}) copy-start(bf16[512,4096]{1,0:T(8,128)(2,1)S(1)} %divide_convert_fusion.scaled_ref.scaled_cols_ref) | copy-start | bytes 12582916
  9.0 15.3 %slice-start = ((s8[8388608]{0:T(1024)(128)(4,1)}), s8[4194304]{0:T(1024)(128)(4,1)S(1)}, s32[]{:S(2)}) async-start(s8[8388608]{0:T(1024)(128)(4,1)} %bitcast.7), calls=%async_computation | async-start | bytes 8388608
  9.3 10.5 %collective-permute-start.1 = (bf16[512,2048]{1,0:T(8,128)(2,1)S(1)}, bf16[512,2048]{1,0:T(8,128)(2,1)S(1)}, u32[]{:S(2)}, u32[]{:S(2)}) collective-permute-start(bf16[512,2048]{1,0:T(8,128)(2,1)S(1)} %slice_select_fusion), channel_id=1, source_target_pairs={{0,1},{4,5},{9,8},{13,12},{18,19},{22,23},{27,26},{31,30}} | collective-permute-start | bytes 6291464 | tf_op jit(solution)/shard_map/ppermute | solution.py:538
  12.1 7.6 %collective-permute-start.2 = (f32[32,2048]{1,0:T(8,128)S(1)}, f32[32,2048]{1,0:T(8,128)S(1)}, u32[]{:S(2)}, u32[]{:S(2)}) collective-permute-start(f32[32,2048]{1,0:T(8,128)S(1)} %broadcast_select_fusion.5), channel_id=1, source_target_pairs={{0,2},{1,3},{2,0},{3,1},{4,6},{5,7},{6,4},{7,5},{8,10},{9,11},{10,... | collective-permute-start | bytes 786440 | tf_op jit(solution)/shard_map/ppermute | solution.py:432
  19.8 4.5 %slice-start.1 = ((s8[8388608]{0:T(1024)(128)(4,1)}), s8[4194304]{0:T(1024)(128)(4,1)S(1)}, s32[]{:S(2)}) async-start(s8[8388608]{0:T(1024)(128)(4,1)} %bitcast.7), calls=%async_computation.1 | async-start | bytes 8388608
  20.5 26.0 %collective-permute-start.11 = (bf16[256,2048]{1,0:T(8,128)(2,1)S(1)}, bf16[256,2048]{1,0:T(8,128)(2,1)S(1)}, u32[]{:S(2)}, u32[]{:S(2)}) collective-permute-start(bf16[256,2048]{1,0:T(8,128)(2,1)S(1)} %slice_select_fusion.1), channel_id=1, source_target_pairs={{0,2},{1,3},{4,6},{5,7},{8,10},{9,11},{12,14},{13,15},{18,16},{19,... | collective-permute-start | bytes 3145736 | tf_op jit(solution)/shard_map/ppermute | solution.py:538
  25.0 18.2 %collective-permute-start.5 = (f32[32,2048]{1,0:T(8,128)S(1)}, f32[32,2048]{1,0:T(8,128)S(1)}, u32[]{:S(2)}, u32[]{:S(2)}) collective-permute-start(f32[32,2048]{1,0:T(8,128)S(1)} %broadcast_select_fusion.4.raw_ref), channel_id=1, source_target_pairs={{0,24},{4,28},{9,1},{13,5},{18,10},{22,14},{27,19},{31,23}} | collective-permute-start | bytes 786440 | tf_op jit(solution)/shard_map/ppermute | solution.py:496
  28.7 14.6 %collective-permute-start.4 = (f32[32,2048]{1,0:T(8,128)S(1)}, f32[32,2048]{1,0:T(8,128)S(1)}, u32[]{:S(2)}, u32[]{:S(2)}) collective-permute-start(f32[32,2048]{1,0:T(8,128)S(1)} %broadcast_select_fusion.4.raw_ref), channel_id=1, source_target_pairs={{0,16},{4,20},{9,25},{13,29},{18,2},{22,6},{27,11},{31,15}} | collective-permute-start | bytes 786440 | tf_op jit(solution)/shard_map/ppermute | solution.py:496
  30.0 13.3 %collective-permute-start.3 = (f32[32,2048]{1,0:T(8,128)S(1)}, f32[32,2048]{1,0:T(8,128)S(1)}, u32[]{:S(2)}, u32[]{:S(2)}) collective-permute-start(f32[32,2048]{1,0:T(8,128)S(1)} %broadcast_select_fusion.4.raw_ref), channel_id=1, source_target_pairs={{0,8},{4,12},{9,17},{13,21},{18,26},{22,30},{27,3},{31,7}} | collective-permute-start | bytes 786440 | tf_op jit(solution)/shard_map/ppermute | solution.py:496
  31.3 1.3 collective-permute-start.7
  32.6 14.2 %collective-permute-start.8 = (bf16[32,512]{1,0:T(8,128)(2,1)S(1)}, bf16[32,512]{1,0:T(8,128)(2,1)S(1)}, u32[]{:S(2)}, u32[]{:S(2)}) collective-permute-start(bf16[32,512]{1,0:T(8,128)(2,1)S(1)} %broadcast_select_fusion.10), channel_id=1, source_target_pairs={{0,2},{1,3},{2,0},{3,1},{4,6},{5,7},{6,4},{7,5},{8,10},{9,11},{10,... | collective-permute-start | bytes 98312 | tf_op jit(solution)/shard_map/ppermute | solution.py:432
  43.4 8.4 %collective-permute-start.6 = (f32[32,2048]{1,0:T(8,128)S(1)}, f32[32,2048]{1,0:T(8,128)S(1)}, u32[]{:S(2)}, u32[]{:S(2)}) collective-permute-start(f32[32,2048]{1,0:T(8,128)S(1)} %add_add_fusion.1), channel_id=1, source_target_pairs={{0,4},{4,0},{8,12},{12,8},{16,20},{20,16},{24,28},{28,24},{1,5},{5... | collective-permute-start | bytes 786440 | tf_op jit(solution)/shard_map/ppermute | solution.py:508
  46.6 11.8 %collective-permute-start.12 = (bf16[256,2048]{1,0:T(8,128)(2,1)S(1)}, bf16[256,2048]{1,0:T(8,128)(2,1)S(1)}, u32[]{:S(2)}, u32[]{:S(2)}) collective-permute-start(bf16[256,2048]{1,0:T(8,128)(2,1)S(1)} %broadcast_select_fusion.1.mine_ref), channel_id=1, source_target_pairs={{0,1},{1,0},{2,3},{3,2},{4,5},{5,4},{6,7},{7,6},{8,9},{9,8},{10,11... | collective-permute-start | bytes 3145736 | tf_op jit(solution)/shard_map/ppermute | solution.py:432
  53.2 1.3 collective-permute-start.9
  54.5 3.9 %collective-permute-start.10 = (f32[64,32]{1,0:T(8,128)S(1)}, f32[64,32]{1,0:T(8,128)S(1)}, u32[]{:S(2)}, u32[]{:S(2)}) collective-permute-start(f32[64,32]{1,0:T(8,128)S(1)} %add.72), channel_id=1, source_target_pairs={{0,2},{1,3},{2,0},{3,1},{4,6},{5,7},{6,4},{7,5},{8,10},{9,11},{10,... | collective-permute-start | bytes 24584 | tf_op jit(solution)/shard_map/ppermute | solution.py:432
  80.4 17.2 %copy-start.1 = (bf16[2048,512]{1,0:T(8,128)(2,1)}, bf16[2048,512]{1,0:T(8,128)(2,1)S(1)}, u32[]{:S(2)}) copy-start(bf16[2048,512]{1,0:T(8,128)(2,1)S(1)} %get-tuple-element.76.turned_ref) | copy-start | bytes 6291460
  80.4 1.5 %collective-permute-start.13 = (f32[32,1312]{1,0:T(8,128)S(1)}, f32[32,1312]{1,0:T(8,128)S(1)}, u32[]{:S(2)}, u32[]{:S(2)}) collective-permute-start(f32[32,1312]{1,0:T(8,128)S(1)} %pad_maximum_fusion.3), channel_id=1, source_target_pairs={{0,1},{1,0},{2,3},{3,2},{4,5},{5,4},{6,7},{7,6},{8,9},{9,8},{10,11... | collective-permute-start | bytes 503816 | tf_op jit(solution)/shard_map/ppermute | solution.py:432
  81.9 6.7 %collective-permute-start.14 = (f32[32,1312]{1,0:T(8,128)S(1)}, f32[32,1312]{1,0:T(8,128)S(1)}, u32[]{:S(2)}, u32[]{:S(2)}) collective-permute-start(f32[32,1312]{1,0:T(8,128)S(1)} %fusion), channel_id=1, source_target_pairs={{0,2},{1,3},{2,0},{3,1},{4,6},{5,7},{6,4},{7,5},{8,10},{9,11},{10,... | collective-permute-start | bytes 503816 | tf_op jit(solution)/shard_map/ppermute | solution.py:432
  88.6 3.8 %collective-permute-start.19 = (f32[32,32]{1,0:T(8,128)S(1)}, f32[32,32]{1,0:T(8,128)S(1)}, u32[]{:S(2)}, u32[]{:S(2)}) collective-permute-start(f32[32,32]{1,0:T(8,128)S(1)} %slice.45), channel_id=1, source_target_pairs={{0,4},{4,0},{8,12},{12,8},{16,20},{20,16},{24,28},{28,24},{1,5},{5... | collective-permute-start | bytes 12296 | tf_op jit(solution)/shard_map/ppermute | solution.py:575
  90.2 2.2 %collective-permute-start.15 = (f32[32,1280]{1,0:T(8,128)S(1)}, f32[32,1280]{1,0:T(8,128)S(1)}, u32[]{:S(2)}, u32[]{:S(2)}) collective-permute-start(f32[32,1280]{1,0:T(8,128)S(1)} %slice.44), channel_id=1, source_target_pairs={{0,1},{1,0},{2,3},{3,2},{4,5},{5,4},{6,7},{7,6},{8,9},{9,8},{10,11... | collective-permute-start | bytes 491528 | tf_op jit(solution)/shard_map/ppermute | solution.py:432
  92.5 24.0 %collective-permute-start.18 = (f32[32,2048]{1,0:T(8,128)S(1)}, f32[32,2048]{1,0:T(8,128)S(1)}, u32[]{:S(2)}, u32[]{:S(2)}) collective-permute-start(f32[32,2048]{1,0:T(8,128)S(1)} %pad_maximum_fusion.2.sums_rows_ref), channel_id=1, source_target_pairs={{0,24},{4,28},{9,1},{13,5},{18,10},{22,14},{27,19},{31,23}} | collective-permute-start | bytes 786440 | tf_op jit(solution)/shard_map/ppermute | solution.py:496
  96.2 20.2 %collective-permute-start.17 = (f32[32,2048]{1,0:T(8,128)S(1)}, f32[32,2048]{1,0:T(8,128)S(1)}, u32[]{:S(2)}, u32[]{:S(2)}) collective-permute-start(f32[32,2048]{1,0:T(8,128)S(1)} %pad_maximum_fusion.2.sums_rows_ref), channel_id=1, source_target_pairs={{0,16},{4,20},{9,25},{13,29},{18,2},{22,6},{27,11},{31,15}} | collective-permute-start | bytes 786440 | tf_op jit(solution)/shard_map/ppermute | solution.py:496
  97.6 18.9 %collective-permute-start.16 = (f32[32,2048]{1,0:T(8,128)S(1)}, f32[32,2048]{1,0:T(8,128)S(1)}, u32[]{:S(2)}, u32[]{:S(2)}) collective-permute-start(f32[32,2048]{1,0:T(8,128)S(1)} %pad_maximum_fusion.2.sums_rows_ref), channel_id=1, source_target_pairs={{0,8},{4,12},{9,17},{13,21},{18,26},{22,30},{27,3},{31,7}} | collective-permute-start | bytes 786440 | tf_op jit(solution)/shard_map/ppermute | solution.py:496
  116.6 7.9 %collective-permute-start.23 = (f32[32,2048]{1,0:T(8,128)S(1)}, f32[32,2048]{1,0:T(8,128)S(1)}, u32[]{:S(2)}, u32[]{:S(2)}) collective-permute-start(f32[32,2048]{1,0:T(8,128)S(1)} %add_add_fusion), channel_id=1, source_target_pairs={{0,4},{4,0},{8,12},{12,8},{16,20},{20,16},{24,28},{28,24},{1,5},{5... | collective-permute-start | bytes 786440 | tf_op jit(solution)/shard_map/ppermute | solution.py:508
  118.1 3.7 %collective-permute-start.22 = (f32[32,32]{1,0:T(8,128)S(1)}, f32[32,32]{1,0:T(8,128)S(1)}, u32[]{:S(2)}, u32[]{:S(2)}) collective-permute-start(f32[32,32]{1,0:T(8,128)S(1)} %slice_add_fusion), channel_id=1, source_target_pairs={{0,24},{4,28},{8,0},{12,4},{16,8},{20,12},{24,16},{28,20},{1,25},{... | collective-permute-start | bytes 12296 | tf_op jit(solution)/shard_map/ppermute | solution.py:584
  118.1 4.6 %collective-permute-start.21 = (f32[32,32]{1,0:T(8,128)S(1)}, f32[32,32]{1,0:T(8,128)S(1)}, u32[]{:S(2)}, u32[]{:S(2)}) collective-permute-start(f32[32,32]{1,0:T(8,128)S(1)} %slice_add_fusion), channel_id=1, source_target_pairs={{0,16},{4,20},{8,24},{12,28},{16,0},{20,4},{24,8},{28,12},{1,17},{... | collective-permute-start | bytes 12296 | tf_op jit(solution)/shard_map/ppermute | solution.py:584
  118.1 6.3 %collective-permute-start.20 = (f32[32,32]{1,0:T(8,128)S(1)}, f32[32,32]{1,0:T(8,128)S(1)}, u32[]{:S(2)}, u32[]{:S(2)}) collective-permute-start(f32[32,32]{1,0:T(8,128)S(1)} %slice_add_fusion), channel_id=1, source_target_pairs={{0,8},{4,12},{8,16},{12,20},{16,24},{20,28},{24,0},{28,4},{1,9},{5... | collective-permute-start | bytes 12296 | tf_op jit(solution)/shard_map/ppermute | solution.py:584

commit v3 on v2

--- a/solution.py
+++ b/solution.py
@@ -1,11 +1,10 @@
-import functools
-
 import jax
 import jax.numpy as jnp
 from jax import lax
 from jax.experimental import pallas as pl
 from jax.experimental.pallas import tpu as pltpu
 from jax.sharding import PartitionSpec as P
+
 
 B = 32
 M = 512
@@ -82,7 +81,7 @@
             out_specs=pl.BlockSpec((B, rows), lambda i, place: (0, 0)),
             scratch_shapes=[pltpu.VMEM((width, rows), F32)],
         ),
-        compiler_params=room(40),
+        compiler_params=room(58),
         name="strip",
     )(place, source)
 
@@ -110,24 +109,27 @@
 
 
 def grow_kernel(turned_ref, scaled_ref, relation_ref, grown_ref):
-    step = relation_ref.shape[0]
+    rows, step = relation_ref.shape
     here = pl.ds(pl.multiple_of(pl.program_id(0) * step, step), step)
-    grown_ref[here, :] = relation_ref[...] + jnp.dot(
-        turned_ref[...], scaled_ref[...], preferred_element_type=F32
-    )
+    chunk = min(512, rows)
+    for k in range(rows // chunk):
+        some = pl.ds(k * chunk, chunk)
+        grown_ref[some, here] = relation_ref[some, :] + jnp.dot(
+            turned_ref[some, :], scaled_ref[...], preferred_element_type=F32
+        )
 
 
 def grow(turned, scaled, relation):
     rows, width = relation.shape
-    step = min(256, rows)
+    step = min(512, width)
     grown = pl.pallas_call(
         grow_kernel,
         out_shape=pltpu.VMEM((rows, width), F32),
-        grid=(rows // step,),
+        grid=(width // step,),
         in_specs=[
-            pl.BlockSpec((step, M), lambda i: (i, 0)),
-            pl.BlockSpec((M, width), lambda i: (0, 0), pipeline_mode=pl.Buffered(1)),
-            pl.BlockSpec((step, width), lambda i: (i, 0)),
+            pl.BlockSpec((rows, M), lambda i: (0, 0), pipeline_mode=pl.Buffered(1)),
+            pl.BlockSpec((M, step), lambda i: (0, i)),
+            pl.BlockSpec((rows, step), lambda i: (0, i)),
         ],
         out_specs=pl.BlockSpec(memory_space=pltpu.VMEM),
         cost_estimate=pl.CostEstimate(
@@ -348,7 +350,7 @@
 def update_kernel(
     triangle_ref, inner_ref, marks_ref, turned_ref, vecs_rows_ref, sums_rows_ref,
     scaled_cols_ref, vecs_cols_ref, sums_cols_ref, relation_ref,
-    out_ref, left_ref, half_ref,
+    out_ref, left_ref, right_ref, half_ref,
 ):
     def dot(a, b, dims):
         return lax.dot_general(a, b, dims, precision=HIGH, preferred_element_type=F32)
@@ -381,12 +383,11 @@
         )
         left = jnp.concatenate([vh, vh, vl, vl, ah, ah, al, al], axis=0)
         left_ref[...] = left.astype(F32).T.astype(BF16)
-
-    scaled = scaled_cols_ref[...]
-    vh, vl, ah, al = parts(
-        vecs_cols_ref[...], sums_cols_ref[...], scaled, NN, 1.0 / M
-    )
-    right = -jnp.concatenate([ah, al, ah, al, vh, vl, vh, vl], axis=0)
+        vh, vl, ah, al = parts(
+            vecs_cols_ref[...], sums_cols_ref[...], scaled_cols_ref[...], NN, 1.0 / M
+        )
+        right_ref[...] = -jnp.concatenate([ah, al, ah, al, vh, vl, vh, vl], axis=0)
+
     rows, step = out_ref.shape
     here = pl.ds(pl.multiple_of(pl.program_id(0) * step, step), step)
     chunk = min(512, rows)
@@ -394,7 +395,7 @@
         some = pl.ds(k * chunk, chunk)
         out_ref[some, :] = (
             relation_ref[some, here]
-            + jnp.dot(left_ref[some, :], right, preferred_element_type=F32)
+            + jnp.dot(left_ref[some, :], right_ref[:, here], preferred_element_type=F32)
         )
 
 
@@ -408,16 +409,19 @@
     def slab(value):
         return pl.BlockSpec((value.shape[0], step), lambda i: (0, i))
 
-    fixed = (triangle, inner, marks) + of_rows
+    fixed = (triangle, inner, marks) + of_rows + of_cols
     return pl.pallas_call(
         update_kernel,
         out_shape=jax.ShapeDtypeStruct((rows, width), F32),
         grid=(width // step,),
         in_specs=[full(value) for value in fixed]
-        + [slab(value) for value in of_cols]
         + [pl.BlockSpec(memory_space=pltpu.VMEM)],
         out_specs=slab(relation),
-        scratch_shapes=[pltpu.VMEM((rows, 8 * B), BF16), pltpu.VMEM((B, B), F32)],
+        scratch_shapes=[
+            pltpu.VMEM((rows, 8 * B), BF16),
+            pltpu.VMEM((8 * B, width), BF16),
+            pltpu.VMEM((B, B), F32),
+        ],
         cost_estimate=pl.CostEstimate(
             flops=16 * B * rows * width,
             bytes_accessed=4 * rows * width,
@@ -425,7 +429,7 @@
         ),
         compiler_params=room(20),
         name="update",
-    )(*fixed, *of_cols, relation)
+    )(*fixed, relation)
 
 
 def swap(value, axis, size, bit):
@@ -514,12 +518,13 @@
             return jnp.concatenate(parts, axis=1)
 
         log_col = n_col.bit_length() - 1
-        raw_rows = from_panel(raw_rows, 0, 1)
-        dosage, raw_rows = lax.optimization_barrier((dosage, raw_rows))
+        chosen = standardize(take_strip(dosage, panel_off), freq, 0)
+        raw_rows, chosen = lax.optimization_barrier((raw_rows, chosen))
+        raw_rows, chosen = from_panel(raw_rows, 0, 1), from_panel(chosen, 0, 1)
+        dosage, raw_rows, chosen = lax.optimization_barrier((dosage, raw_rows, chosen))
         scaled = standardize(dosage, freq)
-        chosen = take_strip(dosage, panel_off)
-        chosen = from_panel(standardize(chosen, freq, 0), 0, log_col)
         raw_rows = from_panel(raw_rows, 1, log_col)
+        chosen = from_panel(chosen, 1, log_col)
 
         own = scaled[:, :tile_rows]
         for k in range(1, per):
@@ -540,7 +545,9 @@
 
         own = spread_rows(own, 1)
         part, _ = halves(own, 0)
-        part, raw_rows, ready = lax.optimization_barrier((part, raw_rows, ready))
+        part, raw_rows, chosen, ready = lax.optimization_barrier(
+            (part, raw_rows, chosen, ready)
+        )
         for bit in bits_of(n_col)[1:]:
             part = spread_rows(part, bit)
         other_part = swap(part, "col", n_col, 1)
@@ -574,10 +581,8 @@
             pairs = [(r, (r // per) * per + (r % per) ^ shift) for r in range(n_row)]
             near = near + lax.ppermute(inner, "row", pairs)
         sums_rows, ready, turned = lax.optimization_barrier((sums_rows, ready, turned))
-        ready, near = lax.optimization_barrier((ready, near))
-        sums_cols, held, near = lax.optimization_barrier(
-            (to_column(sums_rows), grow(turned, scaled, ready), near)
-        )
+        held = grow(turned, scaled, ready)
+        sums_cols, held = lax.optimization_barrier((to_column(sums_rows), held))
         inner = near
         for shift in range(1, n_col):
             pairs = [(r, (r + shift * per) % n_row) for r in range(n_row)]

time: 142 us -> 144 us (1.014)
  waiting for transfers between devices: 31.6 us -> 26.4 us
  starting transfers between devices: 31.7 us -> 34.9 us
  Pallas kernels: 70.9 us -> 74 us
    ppermute x2, waiting for transfers between devices: 5.01 us -> 0.01 us  [join_column(): got.append(lax.ppermute(block, 'row', pairs))]
    ppermute x2, waiting for transfers between devices: 1.49 us -> 4.81 us  [spread_rows(): other = lax.ppermute(value, both, pairs)]
    pallas_call x2, Pallas kernels: 2.8 us -> 5.45 us  [take_strip(): pl.pallas_call(strip_kernel, out_shape=jax.ShapeDtypeStruct((B, rows), F3...]
    ppermute x10, starting transfers between devices: 5.54 us -> 8.06 us  [swap(): return lax.ppermute(value, axis, [(i, i ^ bit) for i in range(size)])]
    ppermute x1, waiting for transfers between devices: 2.13 us -> 0.01 us  [body(): near = near + lax.ppermute(inner, 'row', pairs)]
  transfers between devices with their start and end apart: 24 -> 24, of which waited for: 14 -> 11; matrix products, arithmetic and copies ran while one was open for 0% -> 0% of each run, Pallas kernels for 21% -> 20%
where the time goes in v3:
time: 144 us
  Pallas kernels  74 us (51%)
  starting transfers between devices  34.9 us (24%)
  waiting for transfers between devices  26.4 us (18%)
  other arithmetic  7.07 us (5%)
    pallas_call x1, Pallas kernels, tile_update(): pl.pallas_call(update_kernel, out_shape=jax.ShapeDtypeStruct((rows, width...  17.4 us
    pallas_call x1, Pallas kernels, grow(): pl.pallas_call(grow_kernel, out_shape=pltpu.VMEM((rows, width), F32), gri...  17.4 us
    ppermute x10, waiting for transfers between devices, swap(): return lax.ppermute(value, axis, [(i, i ^ bit) for i in range(size)])  17.4 us
    ppermute x6, starting transfers between devices, to_column(): received.append(lax.ppermute(block, both, pairs))  14.2 us
    pallas_call x1, Pallas kernels, tile_product(): pl.pallas_call(product_kernel, out_shape=(jax.ShapeDtypeStruct((B, width)...  12.8 us
    pallas_call x1, Pallas kernels, hold(): pl.pallas_call(hold_kernel, out_shape=pltpu.VMEM(source.shape, source.dty...  10.6 us
    ppermute x10, starting transfers between devices, swap(): return lax.ppermute(value, axis, [(i, i ^ bit) for i in range(size)])  8.06 us
    pallas_call x1, Pallas kernels, reflect(): pl.pallas_call(reflect_kernel, out_shape=(out,) * 3, compiler_params=room...  7.13 us
  transfers between devices with their start and end apart: 24, of which 11 were waited for; matrix products, arithmetic and copies ran while one was open for 0% of the time, Pallas kernels for 20%

profile of v3, /device:TPU:0, one launch (start us, length us, event | category | flops | bytes accessed | tf_op | source)
XLA Modules:
  0.0 143.6 jit_solution(7832456830035001875)
XLA Ops:
  0.7 0.7 convert_multiply_fusion
  1.4 0.6 pad_add_fusion.1.place_ref
  2.0 2.4 %strip.3 = f32[32,512]{1,0:T(8,128)} custom-call(s32[2]{0:T(128)} %pad_add_fusion.1.place_ref, s32[512,4096]{1,0:T(8,128)} %source_ref.3), custom_call_target="tpu_custom_call" | custom-call | tf_op jit(solution)/shard_map/strip/pallas_call | solution.py:74
  4.4 3.1 %strip.2 = f32[32,2048]{1,0:T(8,128)} custom-call(s32[2]{0:T(128)} %pad_add_fusion.1.place_ref, f32[2048,4096]{1,0:T(8,128)} %relation_ref), custom_call_target="tpu_custom_call" | custom-call | tf_op jit(solution)/shard_map/strip/pallas_call | solution.py:74
  7.5 0.6 collective-permute-start.1
  8.1 0.1 collective-permute-start
  8.1 0.1 pad_add_fusion.place_ref
  8.2 0.7 collective-permute-done.1
  8.9 0.9 collective-permute-done
  9.8 4.4 %divide_convert_fusion.scaled_ref.scaled_cols_ref = bf16[512,4096]{1,0:T(8,128)(2,1)S(1)} fusion(s32[512,4096]{1,0:T(8,128)} %source_ref.3, f32[512]{0:T(512)S(1)} %get-tuple-element.96, f32[512]{0:T(512)S(1)} %get-tuple-element.95), kind=kLoop, calls=%fused_computation | loop fusion | flops 10485760 | bytes 12587008 | tf_op jit(solution)/shard_map/convert_element_type | solution.py:62
  14.2 0.2 slice_select_fusion
  14.5 3.1 %collective-permute-start.2 = (bf16[512,2048]{1,0:T(8,128)(2,1)S(1)}, bf16[512,2048]{1,0:T(8,128)(2,1)S(1)}, u32[]{:S(2)}, u32[]{:S(2)}) collective-permute-start(bf16[512,2048]{1,0:T(8,128)(2,1)S(1)} %slice_select_fusion), channel_id=1, source_target_pairs={{0,1},{4,5},{9,8},{13,12},{18,19},{22,23},{27,26},{31,30}} | collective-permute-start | bytes 6291464 | tf_op jit(solution)/shard_map/ppermute | solution.py:543
  17.6 0.3 collective-permute-start.3
  17.9 1.7 %collective-permute-start.4 = (bf16[32,512]{1,0:T(8,128)(2,1)S(1)}, bf16[32,512]{1,0:T(8,128)(2,1)S(1)}, u32[]{:S(2)}, u32[]{:S(2)}) collective-permute-start(bf16[32,512]{1,0:T(8,128)(2,1)S(1)} %broadcast_select_fusion.11), channel_id=1, source_target_pairs={{0,2},{1,3},{2,0},{3,1},{4,6},{5,7},{6,4},{7,5},{8,10},{9,11},{10,... | collective-permute-start | bytes 98312 | tf_op jit(solution)/shard_map/ppermute | solution.py:436
  19.7 6.8 %collective-permute-done.4 = bf16[32,512]{1,0:T(8,128)(2,1)S(1)} collective-permute-done((bf16[32,512]{1,0:T(8,128)(2,1)S(1)}, bf16[32,512]{1,0:T(8,128)(2,1)S(1)}, u32[]{:S(2)}, u32[]{:S(2)}) %collective-permute-start.4) | collective-permute-done | bytes 32800 | tf_op jit(solution)/shard_map/ppermute | solution.py:436
  26.4 0.0 collective-permute-done.3
  26.5 0.0 collective-permute-done.2
  26.5 0.3 broadcast_select_fusion
  26.8 0.1 slice_select_fusion.1
  26.9 3.0 %collective-permute-start.11 = (bf16[256,2048]{1,0:T(8,128)(2,1)S(1)}, bf16[256,2048]{1,0:T(8,128)(2,1)S(1)}, u32[]{:S(2)}, u32[]{:S(2)}) collective-permute-start(bf16[256,2048]{1,0:T(8,128)(2,1)S(1)} %slice_select_fusion.1), channel_id=1, source_target_pairs={{0,2},{1,3},{4,6},{5,7},{8,10},{9,11},{12,14},{13,15},{18,16},{19,... | collective-permute-start | bytes 3145736 | tf_op jit(solution)/shard_map/ppermute | solution.py:543
  29.9 3.0 %collective-permute-start.7 = (f32[32,2048]{1,0:T(8,128)S(1)}, f32[32,2048]{1,0:T(8,128)S(1)}, u32[]{:S(2)}, u32[]{:S(2)}) collective-permute-start(f32[32,2048]{1,0:T(8,128)S(1)} %broadcast_select_fusion.4.raw_ref), channel_id=1, source_target_pairs={{0,24},{4,28},{9,1},{13,5},{18,10},{22,14},{27,19},{31,23}} | collective-permute-start | bytes 786440 | tf_op jit(solution)/shard_map/ppermute | solution.py:500
  32.9 1.3 collective-permute-start.6
  34.2 1.3 collective-permute-start.5
  35.5 10.6 %hold.1.relation_ref = f32[2048,4096]{1,0:T(8,128)S(1)} custom-call(f32[2048,4096]{1,0:T(8,128)} %relation_ref), custom_call_target="tpu_custom_call" | custom-call | bytes 67108864 | tf_op jit(solution)/shard_map/hold/pallas_call | solution.py:96
  46.1 0.0 collective-permute-done.7
  46.1 0.0 collective-permute-done.6
  46.1 0.0 collective-permute-done.5
  46.1 0.1 add_add_fusion.1
  46.2 1.6 %collective-permute-start.8 = (f32[32,2048]{1,0:T(8,128)S(1)}, f32[32,2048]{1,0:T(8,128)S(1)}, u32[]{:S(2)}, u32[]{:S(2)}) collective-permute-start(f32[32,2048]{1,0:T(8,128)S(1)} %add_add_fusion.1), channel_id=1, source_target_pairs={{0,4},{4,0},{8,12},{12,8},{16,20},{20,16},{24,28},{28,24},{1,5},{5... | collective-permute-start | bytes 786440 | tf_op jit(solution)/shard_map/ppermute | solution.py:512
  47.8 4.8 %collective-permute-done.11 = bf16[256,2048]{1,0:T(8,128)(2,1)S(1)} collective-permute-done((bf16[256,2048]{1,0:T(8,128)(2,1)S(1)}, bf16[256,2048]{1,0:T(8,128)(2,1)S(1)}, u32[]{:S(2)}, u32[]{:S(2)}) %collective-permute-start.11) | collective-permute-done | bytes 1048608 | tf_op jit(solution)/shard_map/ppermute | solution.py:543
  52.6 0.1 broadcast_select_fusion.1.mine_ref
  52.7 0.1 collective-permute-start.12
  52.8 0.0 collective-permute-done.8
  52.9 1.3 panel.1
  54.2 0.6 collective-permute-start.9
  54.8 0.9 collective-permute-done.9
  55.7 2.5 %collective-permute-start.10 = (f32[64,32]{1,0:T(8,128)S(1)}, f32[64,32]{1,0:T(8,128)S(1)}, u32[]{:S(2)}, u32[]{:S(2)}) collective-permute-start(f32[64,32]{1,0:T(8,128)S(1)} %add.72), channel_id=1, source_target_pairs={{0,2},{1,3},{2,0},{3,1},{4,6},{5,7},{6,4},{7,5},{8,10},{9,11},{10,... | collective-permute-start | bytes 24584 | tf_op jit(solution)/shard_map/ppermute | solution.py:436
  58.1 1.9 %collective-permute-done.10 = f32[64,32]{1,0:T(8,128)S(1)} collective-permute-done((f32[64,32]{1,0:T(8,128)S(1)}, f32[64,32]{1,0:T(8,128)S(1)}, u32[]{:S(2)}, u32[]{:S(2)}) %collective-permute-start.10) | collective-permute-done | bytes 8224 | tf_op jit(solution)/shard_map/ppermute | solution.py:436
  60.0 0.0 collective-permute-done.12.other_ref
  60.1 7.1 %reflect.1 = (f32[32,32]{1,0:T(8,128)S(1)}, f32[32,32]{1,0:T(8,128)S(1)}, f32[32,32]{1,0:T(8,128)S(1)}) custom-call(f32[64,32]{1,0:T(8,128)S(1)} %add.73.small_ref), custom_call_target="tpu_custom_call" | custom-call | tf_op jit(solution)/shard_map/reflect/pallas_call | solution.py:345
  67.2 12.8 %product.1 = (f32[32,4096]{1,0:T(8,128)S(1)}, f32[32,2048]{1,0:T(8,128)S(1)}, f32[32,512]{1,0:T(8,128)S(1)}) custom-call(s32[1]{0:T(128)} %bitcast.1.place_ref, f32[32,4096]{1,0:T(8,128)S(1)} %get-tuple-element.70.strip_ref, f32[32,32]{1,0:T(8,128)S(1)} %get-tuple-element.71.factor_ref, f32[32,32]{1,0:T(8,128)S(1)} %get-tuple-element.72.lift_ref, ...), custom_call_target="tpu_custom_call" | custom-call | flops 4294967296 | bytes 33554432 | tf_op jit(solution)/shard_map/product/pallas_call | solution.py:228
  80.1 1.9 %rows.1 = (f32[32,2048]{1,0:T(8,128)S(1)}, f32[32,32]{1,0:T(8,128)S(1)}, bf16[2048,512]{1,0:T(8,128)(2,1)S(1)}) custom-call(s32[2]{0:T(128)S(1)} %pad_add_fusion.place_ref, f32[32,2048]{1,0:T(8,128)S(1)} %broadcast_select_fusion.4.raw_ref, bf16[32,512]{1,0:T(8,128)(2,1)S(1)} %broadcast_select_fusion.10.chosen_ref, ...), custom_call_target="tpu_custom_call" | custom-call | tf_op jit(solution)/shard_map/rows/pallas_call | solution.py:290
  82.0 0.1 collective-permute-start.13
  82.1 1.4 collective-permute-done.13
  83.5 2.1 %collective-permute-start.14 = (f32[32,1312]{1,0:T(8,128)S(1)}, f32[32,1312]{1,0:T(8,128)S(1)}, u32[]{:S(2)}, u32[]{:S(2)}) collective-permute-start(f32[32,1312]{1,0:T(8,128)S(1)} %fusion), channel_id=1, source_target_pairs={{0,2},{1,3},{2,0},{3,1},{4,6},{5,7},{6,4},{7,5},{8,10},{9,11},{10,... | collective-permute-start | bytes 503816 | tf_op jit(solution)/shard_map/ppermute | solution.py:436
  85.6 4.9 %collective-permute-done.14 = f32[32,1312]{1,0:T(8,128)S(1)} collective-permute-done((f32[32,1312]{1,0:T(8,128)S(1)}, f32[32,1312]{1,0:T(8,128)S(1)}, u32[]{:S(2)}, u32[]{:S(2)}) %collective-permute-start.14) | collective-permute-done | bytes 167968 | tf_op jit(solution)/shard_map/ppermute | solution.py:436
  90.5 0.1 collective-permute-start.19
  90.6 1.5 %collective-permute-start.15 = (f32[32,32]{1,0:T(8,128)S(1)}, f32[32,32]{1,0:T(8,128)S(1)}, u32[]{:S(2)}, u32[]{:S(2)}) collective-permute-start(f32[32,32]{1,0:T(8,128)S(1)} %slice.44), channel_id=1, source_target_pairs={{0,4},{4,0},{8,12},{12,8},{16,20},{20,16},{24,28},{28,24},{1,5},{5... | collective-permute-start | bytes 12296 | tf_op jit(solution)/shard_map/ppermute | solution.py:582
  92.1 0.0 collective-permute-done.19
  92.2 5.9 %collective-permute-start.22 = (f32[32,2048]{1,0:T(8,128)S(1)}, f32[32,2048]{1,0:T(8,128)S(1)}, u32[]{:S(2)}, u32[]{:S(2)}) collective-permute-start(f32[32,2048]{1,0:T(8,128)S(1)} %pad_maximum_fusion.2.sums_rows_ref), channel_id=1, source_target_pairs={{0,24},{4,28},{9,1},{13,5},{18,10},{22,14},{27,19},{31,23}} | collective-permute-start | bytes 786440 | tf_op jit(solution)/shard_map/ppermute | solution.py:500
  98.0 1.3 collective-permute-start.21
  99.4 1.5 %collective-permute-start.20 = (f32[32,2048]{1,0:T(8,128)S(1)}, f32[32,2048]{1,0:T(8,128)S(1)}, u32[]{:S(2)}, u32[]{:S(2)}) collective-permute-start(f32[32,2048]{1,0:T(8,128)S(1)} %pad_maximum_fusion.2.sums_rows_ref), channel_id=1, source_target_pairs={{0,8},{4,12},{9,17},{13,21},{18,26},{22,30},{27,3},{31,7}} | collective-permute-start | bytes 786440 | tf_op jit(solution)/shard_map/ppermute | solution.py:500
  100.9 17.4 %grow.1.relation_ref = f32[2048,4096]{1,0:T(8,128)S(1)} custom-call(bf16[2048,512]{1,0:T(8,128)(2,1)} %copy-done.1, bf16[512,4096]{1,0:T(8,128)(2,1)} %copy-done, f32[2048,4096]{1,0:T(8,128)} %relation_ref), custom_call_target="tpu_custom_call" | custom-call | flops 8589934592 | bytes 67108864 | tf_op jit(solution)/shard_map/grow/pallas_call | solution.py:125
  118.3 0.0 collective-permute-done.22
  118.3 0.0 collective-permute-done.20
  118.3 0.1 add_add_fusion
  118.4 1.4 collective-permute-start.23
  119.7 0.0 collective-permute-done.15
  119.7 0.1 collective-permute-start.17
  119.8 1.9 %collective-permute-start.16 = (f32[32,32]{1,0:T(8,128)S(1)}, f32[32,32]{1,0:T(8,128)S(1)}, u32[]{:S(2)}, u32[]{:S(2)}) collective-permute-start(f32[32,32]{1,0:T(8,128)S(1)} %slice_add_fusion), channel_id=1, source_target_pairs={{0,8},{4,12},{8,16},{12,20},{16,24},{20,28},{24,0},{28,4},{1,9},{5... | collective-permute-start | bytes 12296 | tf_op jit(solution)/shard_map/ppermute | solution.py:589
  121.8 1.7 %collective-permute-done.18 = f32[32,32]{1,0:T(8,128)S(1)} collective-permute-done((f32[32,32]{1,0:T(8,128)S(1)}, f32[32,32]{1,0:T(8,128)S(1)}, u32[]{:S(2)}, u32[]{:S(2)}) %collective-permute-start.18) | collective-permute-done | bytes 4128 | tf_op jit(solution)/shard_map/ppermute | solution.py:589
  123.5 1.0 collective-permute-done.17
  124.4 1.6 %collective-permute-done.16 = f32[32,32]{1,0:T(8,128)S(1)} collective-permute-done((f32[32,32]{1,0:T(8,128)S(1)}, f32[32,32]{1,0:T(8,128)S(1)}, u32[]{:S(2)}, u32[]{:S(2)}) %collective-permute-start.16) | collective-permute-done | bytes 4128 | tf_op jit(solution)/shard_map/ppermute | solution.py:589
  126.1 17.4 %update.1 = f32[2048,4096]{1,0:T(8,128)} custom-call(f32[32,32]{1,0:T(8,128)S(1)} %get-tuple-element.69.triangle_ref, f32[32,32]{1,0:T(8,128)S(1)} %add_add_fusion.2.inner_ref, f32[32,512]{1,0:T(8,128)S(1)} %slice.46.marks_ref, bf16[2048,512]{1,0:T(8,128)(2,1)} %copy-done.1, f32[32,2048]{1,0:T(8,128)S(1)} %get-tuple-element.81.vecs_rows_ref, ...), custom_call_target="tpu_custom_call" | custom-call | flops 4294967296 | bytes 33554432 | tf_op jit(solution)/shard_map/update/pallas_call | solution.py:413
  (31 shorter events, 0.4 us)
Async XLA Ops:
  4.4 3.1 %copy-start.2 = (f32[32,512]{1,0:T(8,128)S(1)}, f32[32,512]{1,0:T(8,128)}, u32[]{:S(2)}) copy-start(f32[32,512]{1,0:T(8,128)} %strip.3) | copy-start | bytes 196612
  7.5 1.4 collective-permute-start.1
  8.1 1.7 %collective-permute-start = (f32[32,2048]{1,0:T(8,128)}, f32[32,2048]{1,0:T(8,128)S(1)}, u32[]{:S(2)}, u32[]{:S(2)}) collective-permute-start(f32[32,2048]{1,0:T(8,128)} %strip.2), channel_id=1, source_target_pairs={{0,1},{1,0},{2,3},{3,2},{4,5},{5,4},{6,7},{7,6},{8,9},{9,8},{10,11... | collective-permute-start | bytes 786440 | tf_op jit(solution)/shard_map/ppermute | solution.py:436
  14.2 53.0 %copy-start = (bf16[512,4096]{1,0:T(8,128)(2,1)}, bf16[512,4096]{1,0:T(8,128)(2,1)S(1)}, u32[]{:S(2)}) copy-start(bf16[512,4096]{1,0:T(8,128)(2,1)S(1)} %divide_convert_fusion.scaled_ref.scaled_cols_ref) | copy-start | bytes 12582916
  14.5 12.0 %collective-permute-start.2 = (bf16[512,2048]{1,0:T(8,128)(2,1)S(1)}, bf16[512,2048]{1,0:T(8,128)(2,1)S(1)}, u32[]{:S(2)}, u32[]{:S(2)}) collective-permute-start(bf16[512,2048]{1,0:T(8,128)(2,1)S(1)} %slice_select_fusion), channel_id=1, source_target_pairs={{0,1},{4,5},{9,8},{13,12},{18,19},{22,23},{27,26},{31,30}} | collective-permute-start | bytes 6291464 | tf_op jit(solution)/shard_map/ppermute | solution.py:543
  17.6 8.9 %collective-permute-start.3 = (f32[32,2048]{1,0:T(8,128)S(1)}, f32[32,2048]{1,0:T(8,128)S(1)}, u32[]{:S(2)}, u32[]{:S(2)}) collective-permute-start(f32[32,2048]{1,0:T(8,128)S(1)} %broadcast_select_fusion.5), channel_id=1, source_target_pairs={{0,2},{1,3},{2,0},{3,1},{4,6},{5,7},{6,4},{7,5},{8,10},{9,11},{10,... | collective-permute-start | bytes 786440 | tf_op jit(solution)/shard_map/ppermute | solution.py:436
  17.9 8.5 %collective-permute-start.4 = (bf16[32,512]{1,0:T(8,128)(2,1)S(1)}, bf16[32,512]{1,0:T(8,128)(2,1)S(1)}, u32[]{:S(2)}, u32[]{:S(2)}) collective-permute-start(bf16[32,512]{1,0:T(8,128)(2,1)S(1)} %broadcast_select_fusion.11), channel_id=1, source_target_pairs={{0,2},{1,3},{2,0},{3,1},{4,6},{5,7},{6,4},{7,5},{8,10},{9,11},{10,... | collective-permute-start | bytes 98312 | tf_op jit(solution)/shard_map/ppermute | solution.py:436
  26.9 25.7 %collective-permute-start.11 = (bf16[256,2048]{1,0:T(8,128)(2,1)S(1)}, bf16[256,2048]{1,0:T(8,128)(2,1)S(1)}, u32[]{:S(2)}, u32[]{:S(2)}) collective-permute-start(bf16[256,2048]{1,0:T(8,128)(2,1)S(1)} %slice_select_fusion.1), channel_id=1, source_target_pairs={{0,2},{1,3},{4,6},{5,7},{8,10},{9,11},{12,14},{13,15},{18,16},{19,... | collective-permute-start | bytes 3145736 | tf_op jit(solution)/shard_map/ppermute | solution.py:543
  29.9 16.2 %collective-permute-start.7 = (f32[32,2048]{1,0:T(8,128)S(1)}, f32[32,2048]{1,0:T(8,128)S(1)}, u32[]{:S(2)}, u32[]{:S(2)}) collective-permute-start(f32[32,2048]{1,0:T(8,128)S(1)} %broadcast_select_fusion.4.raw_ref), channel_id=1, source_target_pairs={{0,24},{4,28},{9,1},{13,5},{18,10},{22,14},{27,19},{31,23}} | collective-permute-start | bytes 786440 | tf_op jit(solution)/shard_map/ppermute | solution.py:500
  32.9 13.2 %collective-permute-start.6 = (f32[32,2048]{1,0:T(8,128)S(1)}, f32[32,2048]{1,0:T(8,128)S(1)}, u32[]{:S(2)}, u32[]{:S(2)}) collective-permute-start(f32[32,2048]{1,0:T(8,128)S(1)} %broadcast_select_fusion.4.raw_ref), channel_id=1, source_target_pairs={{0,16},{4,20},{9,25},{13,29},{18,2},{22,6},{27,11},{31,15}} | collective-permute-start | bytes 786440 | tf_op jit(solution)/shard_map/ppermute | solution.py:500
  34.2 11.9 %collective-permute-start.5 = (f32[32,2048]{1,0:T(8,128)S(1)}, f32[32,2048]{1,0:T(8,128)S(1)}, u32[]{:S(2)}, u32[]{:S(2)}) collective-permute-start(f32[32,2048]{1,0:T(8,128)S(1)} %broadcast_select_fusion.4.raw_ref), channel_id=1, source_target_pairs={{0,8},{4,12},{9,17},{13,21},{18,26},{22,30},{27,3},{31,7}} | collective-permute-start | bytes 786440 | tf_op jit(solution)/shard_map/ppermute | solution.py:500
  46.2 6.6 %collective-permute-start.8 = (f32[32,2048]{1,0:T(8,128)S(1)}, f32[32,2048]{1,0:T(8,128)S(1)}, u32[]{:S(2)}, u32[]{:S(2)}) collective-permute-start(f32[32,2048]{1,0:T(8,128)S(1)} %add_add_fusion.1), channel_id=1, source_target_pairs={{0,4},{4,0},{8,12},{12,8},{16,20},{20,16},{24,28},{28,24},{1,5},{5... | collective-permute-start | bytes 786440 | tf_op jit(solution)/shard_map/ppermute | solution.py:512
  52.7 7.3 %collective-permute-start.12 = (bf16[256,2048]{1,0:T(8,128)(2,1)S(1)}, bf16[256,2048]{1,0:T(8,128)(2,1)S(1)}, u32[]{:S(2)}, u32[]{:S(2)}) collective-permute-start(bf16[256,2048]{1,0:T(8,128)(2,1)S(1)} %broadcast_select_fusion.1.mine_ref), channel_id=1, source_target_pairs={{0,1},{1,0},{2,3},{3,2},{4,5},{5,4},{6,7},{7,6},{8,9},{9,8},{10,11... | collective-permute-start | bytes 3145736 | tf_op jit(solution)/shard_map/ppermute | solution.py:436
  54.2 1.4 collective-permute-start.9
  55.7 4.4 %collective-permute-start.10 = (f32[64,32]{1,0:T(8,128)S(1)}, f32[64,32]{1,0:T(8,128)S(1)}, u32[]{:S(2)}, u32[]{:S(2)}) collective-permute-start(f32[64,32]{1,0:T(8,128)S(1)} %add.72), channel_id=1, source_target_pairs={{0,2},{1,3},{2,0},{3,1},{4,6},{5,7},{6,4},{7,5},{8,10},{9,11},{10,... | collective-permute-start | bytes 24584 | tf_op jit(solution)/shard_map/ppermute | solution.py:436
  82.0 17.4 %copy-start.1 = (bf16[2048,512]{1,0:T(8,128)(2,1)}, bf16[2048,512]{1,0:T(8,128)(2,1)S(1)}, u32[]{:S(2)}) copy-start(bf16[2048,512]{1,0:T(8,128)(2,1)S(1)} %get-tuple-element.80.turned_ref) | copy-start | bytes 6291460
  82.0 1.5 %collective-permute-start.13 = (f32[32,1312]{1,0:T(8,128)S(1)}, f32[32,1312]{1,0:T(8,128)S(1)}, u32[]{:S(2)}, u32[]{:S(2)}) collective-permute-start(f32[32,1312]{1,0:T(8,128)S(1)} %pad_maximum_fusion.3), channel_id=1, source_target_pairs={{0,1},{1,0},{2,3},{3,2},{4,5},{5,4},{6,7},{7,6},{8,9},{9,8},{10,11... | collective-permute-start | bytes 503816 | tf_op jit(solution)/shard_map/ppermute | solution.py:436
  83.5 6.9 %collective-permute-start.14 = (f32[32,1312]{1,0:T(8,128)S(1)}, f32[32,1312]{1,0:T(8,128)S(1)}, u32[]{:S(2)}, u32[]{:S(2)}) collective-permute-start(f32[32,1312]{1,0:T(8,128)S(1)} %fusion), channel_id=1, source_target_pairs={{0,2},{1,3},{2,0},{3,1},{4,6},{5,7},{6,4},{7,5},{8,10},{9,11},{10,... | collective-permute-start | bytes 503816 | tf_op jit(solution)/shard_map/ppermute | solution.py:436
  90.5 1.6 %collective-permute-start.19 = (f32[32,1280]{1,0:T(8,128)S(1)}, f32[32,1280]{1,0:T(8,128)S(1)}, u32[]{:S(2)}, u32[]{:S(2)}) collective-permute-start(f32[32,1280]{1,0:T(8,128)S(1)} %slice.45), channel_id=1, source_target_pairs={{0,1},{1,0},{2,3},{3,2},{4,5},{5,4},{6,7},{7,6},{8,9},{9,8},{10,11... | collective-permute-start | bytes 491528 | tf_op jit(solution)/shard_map/ppermute | solution.py:436
  90.6 29.1 %collective-permute-start.15 = (f32[32,32]{1,0:T(8,128)S(1)}, f32[32,32]{1,0:T(8,128)S(1)}, u32[]{:S(2)}, u32[]{:S(2)}) collective-permute-start(f32[32,32]{1,0:T(8,128)S(1)} %slice.44), channel_id=1, source_target_pairs={{0,4},{4,0},{8,12},{12,8},{16,20},{20,16},{24,28},{28,24},{1,5},{5... | collective-permute-start | bytes 12296 | tf_op jit(solution)/shard_map/ppermute | solution.py:582
  92.2 26.1 %collective-permute-start.22 = (f32[32,2048]{1,0:T(8,128)S(1)}, f32[32,2048]{1,0:T(8,128)S(1)}, u32[]{:S(2)}, u32[]{:S(2)}) collective-permute-start(f32[32,2048]{1,0:T(8,128)S(1)} %pad_maximum_fusion.2.sums_rows_ref), channel_id=1, source_target_pairs={{0,24},{4,28},{9,1},{13,5},{18,10},{22,14},{27,19},{31,23}} | collective-permute-start | bytes 786440 | tf_op jit(solution)/shard_map/ppermute | solution.py:500
  98.0 20.2 %collective-permute-start.21 = (f32[32,2048]{1,0:T(8,128)S(1)}, f32[32,2048]{1,0:T(8,128)S(1)}, u32[]{:S(2)}, u32[]{:S(2)}) collective-permute-start(f32[32,2048]{1,0:T(8,128)S(1)} %pad_maximum_fusion.2.sums_rows_ref), channel_id=1, source_target_pairs={{0,16},{4,20},{9,25},{13,29},{18,2},{22,6},{27,11},{31,15}} | collective-permute-start | bytes 786440 | tf_op jit(solution)/shard_map/ppermute | solution.py:500
  99.4 18.9 %collective-permute-start.20 = (f32[32,2048]{1,0:T(8,128)S(1)}, f32[32,2048]{1,0:T(8,128)S(1)}, u32[]{:S(2)}, u32[]{:S(2)}) collective-permute-start(f32[32,2048]{1,0:T(8,128)S(1)} %pad_maximum_fusion.2.sums_rows_ref), channel_id=1, source_target_pairs={{0,8},{4,12},{9,17},{13,21},{18,26},{22,30},{27,3},{31,7}} | collective-permute-start | bytes 786440 | tf_op jit(solution)/shard_map/ppermute | solution.py:500
  118.4 7.7 %collective-permute-start.23 = (f32[32,2048]{1,0:T(8,128)S(1)}, f32[32,2048]{1,0:T(8,128)S(1)}, u32[]{:S(2)}, u32[]{:S(2)}) collective-permute-start(f32[32,2048]{1,0:T(8,128)S(1)} %add_add_fusion), channel_id=1, source_target_pairs={{0,4},{4,0},{8,12},{12,8},{16,20},{20,16},{24,28},{28,24},{1,5},{5... | collective-permute-start | bytes 786440 | tf_op jit(solution)/shard_map/ppermute | solution.py:512
  119.7 3.7 %collective-permute-start.18 = (f32[32,32]{1,0:T(8,128)S(1)}, f32[32,32]{1,0:T(8,128)S(1)}, u32[]{:S(2)}, u32[]{:S(2)}) collective-permute-start(f32[32,32]{1,0:T(8,128)S(1)} %slice_add_fusion), channel_id=1, source_target_pairs={{0,24},{4,28},{8,0},{12,4},{16,8},{20,12},{24,16},{28,20},{1,25},{... | collective-permute-start | bytes 12296 | tf_op jit(solution)/shard_map/ppermute | solution.py:589
  119.7 4.7 %collective-permute-start.17 = (f32[32,32]{1,0:T(8,128)S(1)}, f32[32,32]{1,0:T(8,128)S(1)}, u32[]{:S(2)}, u32[]{:S(2)}) collective-permute-start(f32[32,32]{1,0:T(8,128)S(1)} %slice_add_fusion), channel_id=1, source_target_pairs={{0,16},{4,20},{8,24},{12,28},{16,0},{20,4},{24,8},{28,12},{1,17},{... | collective-permute-start | bytes 12296 | tf_op jit(solution)/shard_map/ppermute | solution.py:589
  119.8 6.2 %collective-permute-start.16 = (f32[32,32]{1,0:T(8,128)S(1)}, f32[32,32]{1,0:T(8,128)S(1)}, u32[]{:S(2)}, u32[]{:S(2)}) collective-permute-start(f32[32,32]{1,0:T(8,128)S(1)} %slice_add_fusion), channel_id=1, source_target_pairs={{0,8},{4,12},{8,16},{12,20},{16,24},{20,28},{24,0},{28,4},{1,9},{5... | collective-permute-start | bytes 12296 | tf_op jit(solution)/shard_map/ppermute | solution.py:589
